TPU v7x, 32 devices: a whole 2x2x4 slice. The times are simulated.
32 devices in a mesh: seq: 8 (over z, x), head: 4 (over y, core).
Axes of the slice: x: 2, y: 2, z: 4, core: 2. Of those that a mesh axis runs over, the one named last changes fastest.
Arguments:
- queries: bfloat16 [6144, 2048], P('seq', 'head'), may hold values from -16 to 16
- key_rows: bfloat16 [6144, 2048], P('seq', 'head'), may hold values from -6 to 6
- value_rows: bfloat16 [6144, 2048], P('seq', 'head'), may hold values from -6 to 6
- out_weight: bfloat16 [2048, 3072], P('head'), may hold values from -0.125 to 0.125
- cotangent: bfloat16 [6144, 3072], P('seq', 'head'), may hold values from -6 to 6
- neighbours: int32 [16, 4], P('seq'), may hold values from -1 to 15, as said below
Outputs:
- projected: bfloat16 [6144, 3072], P('seq', 'head')
- grad_queries: bfloat16 [6144, 2048], P('seq', 'head')
- grad_keys: bfloat16 [6144, 2048], P('seq', 'head')
- grad_values: bfloat16 [6144, 2048], P('seq', 'head')
- grad_weight: float32 [2048, 3072], P('head', 'seq')
Inputs may be any that keep to these rules, and one draw needn't show every extreme that they name: `neighbours`: slot 0 of tile t holds t; every other slot holds -1 or a tile other than t within 2 tiles of t, no tile twice in a row; the -1 slots of a row come after its tiles.
All inputs are finite; a program needn't handle non-finite values.
Results may differ from a plain program's by a relative error of at most 0.014.
Values may be sent and summed in bfloat16 or wider, within the bound.
A program may use at most 192 MiB of HBM per device.

v0:
```python
import functools
import math

import jax
import jax.numpy as jnp
from jax import lax
from jax.experimental import pallas as pl
from jax.experimental.pallas import tpu as pltpu
from jax.sharding import PartitionSpec as P

HD = 128
TILE = 384
REACH = 2
SLOTS = 4
RIM = REACH * TILE
F32 = jnp.float32
BF16 = jnp.bfloat16


def dot_nt(a, b):
    return lax.dot_general(a, b, (((1,), (1,)), ((), ())), preferred_element_type=F32)


def dot_nn(a, b):
    return lax.dot_general(a, b, (((1,), (0,)), ((), ())), preferred_element_type=F32)


def dot_tn(a, b):
    return lax.dot_general(a, b, (((0,), (0,)), ((), ())), preferred_element_type=F32)


def fold(op, x):
    out = x[:, :HD]
    for i in range(1, x.shape[1] // HD):
        out = op(out, x[:, i * HD : (i + 1) * HD])
    return out


def attend(rows, tiles, place, count, q, g, km, vm, far, near, att, dq, mid, rim_far, rim_near, kx, vx, dk, dv, scr):
    t = pl.program_id(1)
    scale = 1.0 / math.sqrt(HD)
    c = scale * math.log2(math.e)
    hi = RIM + rows

    @pl.when(t == 0)
    def _():
        kx[:RIM] = far[0]
        kx[RIM:hi] = km[...]
        kx[hi:] = near[0]
        vx[:RIM] = far[1]
        vx[RIM:hi] = vm[...]
        vx[hi:] = near[1]
        dk[...] = jnp.zeros_like(dk)
        dv[...] = jnp.zeros_like(dv)

    live = count[t]
    qv = q[...]
    gv = g[...]

    def at(j):
        return pl.ds(pl.multiple_of(place[t * SLOTS + j] * TILE, TILE), TILE)

    def score(j, m):
        s = dot_nt(qv, kx[at(j), :])
        scr[j] = s
        return jnp.maximum(m, fold(jnp.maximum, s))

    m = lax.fori_loop(0, live, score, jnp.full((TILE, HD), -3e38, F32))
    m = jnp.max(m, axis=1, keepdims=True)

    def soft(j, carry):
        total, acc = carry
        e = jnp.exp2((scr[j] - m) * c)
        scr[j] = e
        return total + fold(jnp.add, e), acc + dot_nn(e.astype(BF16), vx[at(j), :])

    zero = jnp.zeros((TILE, HD), F32)
    total, acc = lax.fori_loop(0, live, soft, (zero, zero))
    inv = 1.0 / jnp.sum(total, axis=1, keepdims=True)
    out = (acc * inv).astype(BF16)
    att[...] = out
    delta = jnp.sum(gv.astype(F32) * out.astype(F32), axis=1, keepdims=True)

    def back(j, acc):
        here = at(j)
        k = kx[here, :]
        p = scr[j] * inv
        ds = (p * (dot_nt(gv, vx[here, :]) - delta)).astype(BF16)
        dv[here, :] += dot_tn(p.astype(BF16), gv)
        dk[here, :] += dot_tn(ds, qv)
        return acc + dot_nn(ds, k)

    dq[...] = (lax.fori_loop(0, live, back, zero) * scale).astype(BF16)

    @pl.when(t == tiles - 1)
    def _():
        rim_far[0] = (dk[:RIM] * scale).astype(BF16)
        rim_far[1] = dv[:RIM].astype(BF16)
        mid[0] = dk[RIM:hi] * scale
        mid[1] = dv[RIM:hi]
        rim_near[0] = dk[hi:] * scale
        rim_near[1] = dv[hi:]


def attention_call(place, count, q, g, k, v, far, near, first, heads):
    rows = q.shape[0]
    tiles = rows // TILE
    ext = rows + 2 * RIM
    cols = heads * HD
    tile_in = pl.BlockSpec((TILE, HD), lambda h, t, *_: (t, first + h))
    slab_in = pl.BlockSpec((rows, HD), lambda h, t, *_: (0, first + h))
    rim = pl.BlockSpec((2, RIM, HD), lambda h, t, *_: (0, 0, h))
    tile_out = pl.BlockSpec((TILE, HD), lambda h, t, *_: (t, h))
    mid = pl.BlockSpec((2, rows, HD), lambda h, t, *_: (0, 0, h))
    pairs = heads * tiles * SLOTS
    return pl.pallas_call(
        functools.partial(attend, rows, tiles),
        grid_spec=pltpu.PrefetchScalarGridSpec(
            num_scalar_prefetch=2,
            grid=(heads, tiles),
            in_specs=[tile_in, tile_in, slab_in, slab_in, rim, rim],
            out_specs=[tile_out, tile_out, mid, rim, rim],
            scratch_shapes=[
                pltpu.VMEM((ext, HD), BF16),
                pltpu.VMEM((ext, HD), BF16),
                pltpu.VMEM((ext, HD), F32),
                pltpu.VMEM((ext, HD), F32),
                pltpu.VMEM((SLOTS, TILE, TILE), F32),
            ],
        ),
        out_shape=[
            jax.ShapeDtypeStruct((rows, cols), BF16),
            jax.ShapeDtypeStruct((rows, cols), BF16),
            jax.ShapeDtypeStruct((2, rows, cols), F32),
            jax.ShapeDtypeStruct((2, RIM, cols), BF16),
            jax.ShapeDtypeStruct((2, RIM, cols), F32),
        ],
        compiler_params=pltpu.CompilerParams(
            dimension_semantics=("arbitrary", "arbitrary"), vmem_limit_bytes=40 << 20
        ),
        cost_estimate=pl.CostEstimate(
            flops=pairs * 12 * TILE * TILE * HD,
            bytes_accessed=rows * cols * 40,
            transcendentals=pairs * TILE * TILE,
        ),
    )(place, count, q, g, k, v, far, near)


def swap(x, axis, bit):
    return lax.ppermute(x, axis, [(i, i ^ bit) for i in range(lax.axis_size(axis))])


def shift(x, axis, even_step):
    size = lax.axis_size(axis)
    pairs = [(i, i + (even_step if i % 2 == 0 else -even_step)) for i in range(size)]
    return lax.ppermute(x, axis, [(i, j) for i, j in pairs if 0 <= j < size])


def local(queries, key_rows, value_rows, out_weight, cotangent, neighbours):
    rows, columns = queries.shape
    heads = columns // HD
    tiles = rows // TILE
    seq, head = lax.axis_size("seq"), lax.axis_size("head")
    s, h = lax.axis_index("seq"), lax.axis_index("head")
    paired = head == 4 and seq == 8
    width = cotangent.shape[1]
    piece = width * head // seq
    norm = 1.0 / math.sqrt(rows * seq)
    chunks = 2
    per = heads // chunks

    halos = []
    for n in range(chunks):
        cut = slice(n * per * HD, (n + 1) * per * HD)
        kv = jnp.stack([key_rows[:, cut], value_rows[:, cut]])
        near = swap(kv, "seq", 1)
        far = shift(near, "seq", 2)
        halos.append((far, near))

    if paired:
        shards = [cotangent, swap(cotangent, "head", 1), swap(cotangent, "head", 2)]
        shards.append(swap(shards[2], "head", 1))
        weights = [
            lax.dynamic_slice_in_dim(out_weight, (h ^ r) * width, width, 1) for r in range(4)
        ]
        grad_attention = sum(dot_nt(a, b) for a, b in zip(shards, weights)).astype(BF16)
    else:
        full = lax.all_gather(cotangent, "head", axis=1, tiled=True)
        grad_attention = dot_nt(full, out_weight).astype(BF16)

    first = s * tiles - REACH
    alive = neighbours >= 0
    index = jnp.where(alive, neighbours - first, 0)
    span = tiles + REACH
    odd = s % 2 == 1
    turned = jnp.where(index < REACH, index + span, jnp.where(index >= span, index - span, index))
    place = jnp.where(odd, turned, index).reshape(-1).astype(jnp.int32)
    count = jnp.sum(alive, axis=1).astype(jnp.int32)

    atts, dqs, dks, dvs, gws = [], [], [], [], []
    for n in range(chunks):
        far, near = halos[n]
        att, dq, mid, rim_far, rim_near = attention_call(
            place, count, queries, grad_attention, key_rows, value_rows, far, near, n * per, per
        )
        relayed = shift(rim_far, "seq", -2)
        back = swap((rim_near + relayed.astype(F32)).astype(BF16), "seq", 1)
        done = (mid + back.astype(F32)).astype(BF16)
        atts.append(att)
        dqs.append(dq)
        dks.append(done[0])
        dvs.append(done[1])

    attention = jnp.concatenate(atts, axis=1)
    if paired:
        parts = [dot_nn(attention, w) for w in weights]
        sent = jnp.stack([parts[1], parts[3]]).astype(BF16)
        got = swap(sent, "head", 1).astype(F32)
        other = swap((parts[2] + got[1]).astype(BF16), "head", 2)
        projected = (parts[0] + got[0] + other.astype(F32)).astype(BF16)
        stacked = jnp.stack(shards)
        z, x = s // 2, s % 2
        turn = h ^ z

        def columns_of(k, side):
            block = lax.dynamic_index_in_dim(stacked, turn ^ k, 0, False)
            return lax.dynamic_slice_in_dim(block, side * piece, piece, 1)

        send = jnp.stack([columns_of(k, 1 - x) for k in range(4)])
        keep = jnp.stack([columns_of(k, x) for k in range(4)])
        away = jnp.einsum("tc,ktd->kcd", attention, send, preferred_element_type=F32)
        stay = jnp.einsum("tc,ktd->kcd", attention, keep, preferred_element_type=F32)
        stay = stay + swap(away.astype(BF16), "seq", 1).astype(F32)
        got = swap(jnp.stack([stay[1], stay[3]]).astype(BF16), "seq", 2).astype(F32)
        last = swap((stay[2] + got[1]).astype(BF16), "seq", 4).astype(F32)
        grad_weight = (stay[0] + got[0] + last) * norm
    else:
        projected = lax.psum_scatter(
            dot_nn(attention, out_weight).astype(BF16), "head", scatter_dimension=1, tiled=True
        )
        grad_weight = (
            lax.psum_scatter(
                dot_tn(attention, full).astype(BF16), "seq", scatter_dimension=1, tiled=True
            ).astype(F32)
            * norm
        )
    return (
        projected,
        jnp.concatenate(dqs, axis=1),
        jnp.concatenate(dks, axis=1),
        jnp.concatenate(dvs, axis=1),
        grad_weight,
    )


def solution(mesh):
    both = P("seq", "head")
    return jax.shard_map(
        local,
        mesh=mesh,
        in_specs=(both, both, both, P("head", None), both, P("seq", None)),
        out_specs=(both, both, both, both, P("head", "seq")),
        check_vma=False,
    )
```

profile of v0, /device:TPU:0, one launch (start us, length us, event | category | flops | bytes accessed | tf_op | source)
XLA Modules:
  0.0 211.2 jit_solution(6893286039921164687)
XLA Ops:
  0.6 2.5 %copy.11 = bf16[768,768]{0,1:T(8,128)(2,1)} copy(bf16[768,768]{1,0:T(8,128)(2,1)} %param.10) | data formatting | bytes 2359296 | tf_op args[4]
  3.2 3.0 %collective-permute-start.1 = (bf16[768,768]{0,1:T(8,128)(2,1)}, bf16[768,768]{0,1:T(8,128)(2,1)}, u32[]{:S(2)}, u32[]{:S(2)}) collective-permute-start(bf16[768,768]{0,1:T(8,128)(2,1)} %copy.11), channel_id=1, source_target_pairs={{0,2},{1,3},{2,0},{3,1},{4,6},{5,7},{6,4},{7,5},{8,10},{9,11},{10,... | collective-permute-start | bytes 3538952 | tf_op jit(solution)/shard_map/ppermute | solution.py:150
  6.1 1.5 slice_bitcast_fusion.6
  7.6 0.9 pad_maximum_fusion.2
  8.6 1.5 collective-permute-start.3
  10.1 0.9 pad_maximum_fusion.3
  11.0 0.5 collective-permute-start.5
  11.5 20.9 %collective-permute-done.1 = bf16[768,768]{0,1:T(8,128)(2,1)} collective-permute-done((bf16[768,768]{0,1:T(8,128)(2,1)}, bf16[768,768]{0,1:T(8,128)(2,1)}, u32[]{:S(2)}, u32[]{:S(2)}) %collective-permute-start.1) | collective-permute-done | bytes 1179680 | tf_op jit(solution)/shard_map/ppermute | solution.py:150
  32.6 2.1 fusion.47
  34.7 3.8 %collective-permute-start.4 = (bf16[2,768,256]{2,1,0:T(8,128)(2,1)}, bf16[2,768,256]{2,1,0:T(8,128)(2,1)S(1)}, u32[]{:S(2)}, u32[]{:S(2)}) collective-permute-start(bf16[2,768,256]{2,1,0:T(8,128)(2,1)} %collective-permute-done.3.near), channel_id=1, source_target_pairs={{0,8},{8,16},{12,4},{16,24},{20,12},{28,20},{1,9},{9,17},{13,5},{1... | collective-permute-start | bytes 2359304 | tf_op jit(solution)/shard_map/ppermute | solution.py:156
  38.5 7.2 %collective-permute-done.5.near = bf16[2,768,256]{2,1,0:T(8,128)(2,1)} collective-permute-done((bf16[2,768,256]{2,1,0:T(8,128)(2,1)}, bf16[2,768,256]{2,1,0:T(8,128)(2,1)}, u32[]{:S(2)}, u32[]{:S(2)}) %collective-permute-start.5) | collective-permute-done | bytes 786464 | tf_op jit(solution)/shard_map/ppermute | solution.py:150
  45.7 3.5 %collective-permute-start.6 = (bf16[2,768,256]{2,1,0:T(8,128)(2,1)}, bf16[2,768,256]{2,1,0:T(8,128)(2,1)S(1)}, u32[]{:S(2)}, u32[]{:S(2)}) collective-permute-start(bf16[2,768,256]{2,1,0:T(8,128)(2,1)} %collective-permute-done.5.near), channel_id=1, source_target_pairs={{0,8},{8,16},{12,4},{16,24},{20,12},{28,20},{1,9},{9,17},{13,5},{1... | collective-permute-start | bytes 2359304 | tf_op jit(solution)/shard_map/ppermute | solution.py:156
  49.2 2.1 fusion.41
  51.3 2.1 fusion.44
  53.5 2.3 %fusion.31.g = bf16[768,512]{1,0:T(8,128)(2,1)S(1)} fusion(bf16[768,768]{0,1:T(8,128)(2,1)} %collective-permute-done.2, f32[512,768]{0,1:T(8,128)S(1)} %fusion.41, f32[512,768]{0,1:T(8,128)S(1)} %fusion.47, f32[512,768]{0,1:T(8,128)S(1)} %fusion.44, bf16[512,3072]{1,0:T(8,128)(2,1)S(1)} %copy-done, s32[]{:T(128)S(6)} %select_n.94), kind=kOutput, calls=%fused_computation.37 | convolution fusion | flops 605552640 | bytes 7471108 | tf_op jit(solution)/shard_map/dot_general | solution.py:21
  55.7 0.8 collective-permute-done.4.far
  56.6 21.6 %shard_map.101 = (bf16[768,256]{1,0:T(8,128)(2,1)S(1)}, bf16[768,256]{1,0:T(8,128)(2,1)S(1)}, f32[2,768,256]{2,1,0:T(8,128)S(1)}, bf16[2,768,256]{2,1,0:T(8,128)(2,1)S(1)}, f32[2,768,256]{2,1,0:T(8,128)S(1)}) custom-call(s32[8]{0:T(128)S(1)} %reshape.32.place, s32[2]{0:T(128)S(1)} %get-tuple-element.48.count, bf16[768,512]{1,0:T(8,128)(2,1)S(1)} %copy-done.3, ...), custom_call_target="tpu_custom_call" | custom-call | flops 3623878656 | bytes 7864320 | tf_op jit(solution)/shard_map/pallas_call | solution.py:116
  78.2 21.7 %shard_map.102 = (bf16[768,256]{1,0:T(8,128)(2,1)S(1)}, bf16[768,256]{1,0:T(8,128)(2,1)S(1)}, f32[2,768,256]{2,1,0:T(8,128)S(1)}, bf16[2,768,256]{2,1,0:T(8,128)(2,1)S(1)}, f32[2,768,256]{2,1,0:T(8,128)S(1)}) custom-call(s32[8]{0:T(128)S(1)} %reshape.32.place, s32[2]{0:T(128)S(1)} %get-tuple-element.48.count, bf16[768,512]{1,0:T(8,128)(2,1)S(1)} %copy-done.3, ...), custom_call_target="tpu_custom_call" | custom-call | flops 3623878656 | bytes 7864320 | tf_op jit(solution)/shard_map/pallas_call | solution.py:116
  100.0 2.5 %pad_maximum_fusion = bf16[4,768,768]{1,2,0:T(8,128)(2,1)S(1)} fusion(bf16[1,768,768]{1,2,0:T(8,128)(2,1)} %bitcast.16, bf16[1,768,768]{1,2,0:T(8,128)(2,1)} %bitcast.15, bf16[1,768,768]{1,2,0:T(8,128)(2,1)} %bitcast.14, bf16[1,768,768]{1,2,0:T(8,128)(2,1)S(1)} %bitcast.67), kind=kLoop, calls=%fused_computation | loop fusion | flops 7077888 | bytes 9437184 | tf_op jit(solution)/shard_map/stack | solution.py:221
  102.6 1.1 constant_dynamic-slice_fusion.7
  103.7 1.4 fusion.26
  105.1 2.4 %collective-permute-start.13 = (bf16[4,512,384]{1,2,0:T(8,128)(2,1)S(1)}, bf16[4,512,384]{1,2,0:T(8,128)(2,1)S(1)}, u32[]{:S(2)}, u32[]{:S(2)}) collective-permute-start(bf16[4,512,384]{1,2,0:T(8,128)(2,1)S(1)} %fusion.26), channel_id=1, source_target_pairs={{0,4},{4,0},{8,12},{12,8},{16,20},{20,16},{24,28},{28,24},{1,5},{5... | collective-permute-start | bytes 4718600 | tf_op jit(solution)/shard_map/ppermute | solution.py:150
  107.5 1.3 collective-permute-start.11
  108.8 1.5 collective-permute-start.9
  110.3 0.8 fusion.30
  111.1 0.8 fusion.29
  111.9 0.2 pad_maximum_fusion.1
  112.2 0.9 pad_maximum_fusion.4
  113.1 21.0 %collective-permute-done.11 = bf16[2,768,256]{2,1,0:T(8,128)(2,1)S(1)} collective-permute-done((bf16[2,768,256]{2,1,0:T(8,128)(2,1)S(1)}, bf16[2,768,256]{2,1,0:T(8,128)(2,1)S(1)}, u32[]{:S(2)}, u32[]{:S(2)}) %collective-permute-start.11) | collective-permute-done | bytes 786464 | tf_op jit(solution)/shard_map/ppermute | solution.py:156
  134.1 0.2 add_convert_fusion.1
  134.5 14.8 %collective-permute-done.9 = bf16[2,768,256]{2,1,0:T(8,128)(2,1)S(1)} collective-permute-done((bf16[2,768,256]{2,1,0:T(8,128)(2,1)S(1)}, bf16[2,768,256]{2,1,0:T(8,128)(2,1)S(1)}, u32[]{:S(2)}, u32[]{:S(2)}) %collective-permute-start.9) | collective-permute-done | bytes 786464 | tf_op jit(solution)/shard_map/ppermute | solution.py:156
  149.3 0.2 add_convert_fusion.3
  149.6 1.4 fusion.62
  151.2 2.1 collective-permute-start.14
  153.3 6.3 %collective-permute-done.12 = bf16[2,768,256]{2,1,0:T(8,128)(2,1)S(1)} collective-permute-done((bf16[2,768,256]{2,1,0:T(8,128)(2,1)S(1)}, bf16[2,768,256]{2,1,0:T(8,128)(2,1)S(1)}, u32[]{:S(2)}, u32[]{:S(2)}) %collective-permute-start.12) | collective-permute-done | bytes 786464 | tf_op jit(solution)/shard_map/ppermute | solution.py:150
  159.8 15.3 %collective-permute-done.10 = bf16[2,768,256]{2,1,0:T(8,128)(2,1)S(1)} collective-permute-done((bf16[2,768,256]{2,1,0:T(8,128)(2,1)S(1)}, bf16[2,768,256]{2,1,0:T(8,128)(2,1)S(1)}, u32[]{:S(2)}, u32[]{:S(2)}) %collective-permute-start.10) | collective-permute-done | bytes 786464 | tf_op jit(solution)/shard_map/ppermute | solution.py:150
  175.1 0.2 add_convert_fusion.2
  175.4 0.4 convert_element_type.70
  175.8 2.3 %fusion.1 = bf16[768,768]{1,0:T(8,128)(2,1)} fusion(f32[2,768,768]{2,1,0:T(8,128)S(1)} %convert_element_type.70, bf16[768,512]{1,0:T(8,128)(2,1)S(1)} %constant_dynamic-update-slice_fusion, bf16[512,3072]{1,0:T(8,128)(2,1)S(1)} %copy-done, s32[]{:T(128)S(6)} %select_n.93), kind=kOutput, calls=%fused_computation.4 | convolution fusion | flops 605159424 | bytes 5111812 | tf_op jit(solution)/shard_map/dot_general | solution.py:25
  178.1 0.3 copy-done.4
  178.3 1.5 collective-permute-start.8
  180.3 7.4 %collective-permute-start.15 = (bf16[512,384]{0,1:T(8,128)(2,1)S(1)}, bf16[512,384]{0,1:T(8,128)(2,1)S(1)}, u32[]{:S(2)}, u32[]{:S(2)}) collective-permute-start(bf16[512,384]{0,1:T(8,128)(2,1)S(1)} %fusion.49), channel_id=1, source_target_pairs={{0,16},{4,20},{8,24},{12,28},{16,0},{20,4},{24,8},{28,12},{1,17},{... | collective-permute-start | bytes 1179656 | tf_op jit(solution)/shard_map/ppermute | solution.py:150
  187.7 0.9 pad_maximum_fusion.6
  188.6 0.9 pad_maximum_fusion.5
  189.6 14.2 %collective-permute-done.15 = bf16[512,384]{0,1:T(8,128)(2,1)S(1)} collective-permute-done((bf16[512,384]{0,1:T(8,128)(2,1)S(1)}, bf16[512,384]{0,1:T(8,128)(2,1)S(1)}, u32[]{:S(2)}, u32[]{:S(2)}) %collective-permute-start.15) | collective-permute-done | bytes 393248 | tf_op jit(solution)/shard_map/ppermute | solution.py:150
  203.8 1.1 fusion.35
  204.9 2.3 %copy.18 = f32[512,384]{1,0:T(8,128)} copy(f32[512,384]{0,1:T(8,128)} %fusion.35) | data formatting | bytes 1572864
  207.1 4.0 %fusion.4 = bf16[768,768]{1,0:T(8,128)(2,1)} fusion(f32[2,768,768]{2,1,0:T(8,128)} %copy-done.4, bf16[768,768]{1,0:T(8,128)(2,1)} %collective-permute-done.8, bf16[768,512]{1,0:T(8,128)(2,1)} %copy-done.5, bf16[512,3072]{1,0:T(8,128)(2,1)S(1)} %copy-done, s32[]{:T(128)S(6)} %select_n.91), kind=kOutput, calls=%fused_computation.8 | convolution fusion | flops 606339072 | bytes 6291460 | tf_op jit(solution)/shard_map/dot_general | solution.py:25
  (39 shorter events, 1.3 us)
Async XLA Ops:
  0.6 32.0 %copy-start = (bf16[512,3072]{1,0:T(8,128)(2,1)S(1)}, bf16[512,3072]{1,0:T(8,128)(2,1)}, u32[]{:S(2)}) copy-start(bf16[512,3072]{1,0:T(8,128)(2,1)} %param.9) | copy-start | bytes 9437188
  3.2 29.2 %collective-permute-start.1 = (bf16[768,768]{0,1:T(8,128)(2,1)}, bf16[768,768]{0,1:T(8,128)(2,1)}, u32[]{:S(2)}, u32[]{:S(2)}) collective-permute-start(bf16[768,768]{0,1:T(8,128)(2,1)} %copy.11), channel_id=1, source_target_pairs={{0,2},{1,3},{2,0},{3,1},{4,6},{5,7},{6,4},{7,5},{8,10},{9,11},{10,... | collective-permute-start | bytes 3538952 | tf_op jit(solution)/shard_map/ppermute | solution.py:150
  6.1 45.2 %collective-permute-start = (bf16[768,768]{0,1:T(8,128)(2,1)}, bf16[768,768]{0,1:T(8,128)(2,1)}, u32[]{:S(2)}, u32[]{:S(2)}) collective-permute-start(bf16[768,768]{0,1:T(8,128)(2,1)} %copy.11), channel_id=1, source_target_pairs={{0,1},{1,0},{2,3},{3,2},{4,5},{5,4},{6,7},{7,6},{8,9},{9,8},{10,11... | collective-permute-start | bytes 3538952 | tf_op jit(solution)/shard_map/ppermute | solution.py:150
  7.6 24.8 %copy-start.7 = (s32[2,4]{1,0:T(2,128)S(1)}, s32[2,4]{1,0:T(2,128)}, u32[]{:S(2)}) copy-start(s32[2,4]{1,0:T(2,128)} %param.11) | copy-start | bytes 100
  8.6 26.2 %collective-permute-start.3 = (bf16[2,768,256]{2,1,0:T(8,128)(2,1)}, bf16[2,768,256]{2,1,0:T(8,128)(2,1)}, u32[]{:S(2)}, u32[]{:S(2)}) collective-permute-start(bf16[2,768,256]{2,1,0:T(8,128)(2,1)} %pad_maximum_fusion.2), channel_id=1, source_target_pairs={{0,4},{4,0},{8,12},{12,8},{16,20},{20,16},{24,28},{28,24},{1,5},{5... | collective-permute-start | bytes 2359304 | tf_op jit(solution)/shard_map/ppermute | solution.py:150
  11.0 34.7 %collective-permute-start.5 = (bf16[2,768,256]{2,1,0:T(8,128)(2,1)}, bf16[2,768,256]{2,1,0:T(8,128)(2,1)}, u32[]{:S(2)}, u32[]{:S(2)}) collective-permute-start(bf16[2,768,256]{2,1,0:T(8,128)(2,1)} %pad_maximum_fusion.3), channel_id=1, source_target_pairs={{0,4},{4,0},{8,12},{12,8},{16,20},{20,16},{24,28},{28,24},{1,5},{5... | collective-permute-start | bytes 2359304 | tf_op jit(solution)/shard_map/ppermute | solution.py:150
  32.4 21.1 %collective-permute-start.2 = (bf16[768,768]{0,1:T(8,128)(2,1)}, bf16[768,768]{0,1:T(8,128)(2,1)}, u32[]{:S(2)}, u32[]{:S(2)}) collective-permute-start(bf16[768,768]{0,1:T(8,128)(2,1)} %collective-permute-done.1), channel_id=1, source_target_pairs={{0,1},{1,0},{2,3},{3,2},{4,5},{5,4},{6,7},{7,6},{8,9},{9,8},{10,11... | collective-permute-start | bytes 3538952 | tf_op jit(solution)/shard_map/ppermute | solution.py:150
  34.7 21.9 %collective-permute-start.4 = (bf16[2,768,256]{2,1,0:T(8,128)(2,1)}, bf16[2,768,256]{2,1,0:T(8,128)(2,1)S(1)}, u32[]{:S(2)}, u32[]{:S(2)}) collective-permute-start(bf16[2,768,256]{2,1,0:T(8,128)(2,1)} %collective-permute-done.3.near), channel_id=1, source_target_pairs={{0,8},{8,16},{12,4},{16,24},{20,12},{28,20},{1,9},{9,17},{13,5},{1... | collective-permute-start | bytes 2359304 | tf_op jit(solution)/shard_map/ppermute | solution.py:156
  45.7 32.5 %collective-permute-start.6 = (bf16[2,768,256]{2,1,0:T(8,128)(2,1)}, bf16[2,768,256]{2,1,0:T(8,128)(2,1)S(1)}, u32[]{:S(2)}, u32[]{:S(2)}) collective-permute-start(bf16[2,768,256]{2,1,0:T(8,128)(2,1)} %collective-permute-done.5.near), channel_id=1, source_target_pairs={{0,8},{8,16},{12,4},{16,24},{20,12},{28,20},{1,9},{9,17},{13,5},{1... | collective-permute-start | bytes 2359304 | tf_op jit(solution)/shard_map/ppermute | solution.py:156
  53.4 3.2 %copy-start.1 = (bf16[768,512]{1,0:T(8,128)(2,1)S(1)}, bf16[768,512]{1,0:T(8,128)(2,1)}, u32[]{:S(2)}) copy-start(bf16[768,512]{1,0:T(8,128)(2,1)} %km.3) | copy-start | bytes 2359300
  53.4 3.1 %copy-start.2 = (bf16[768,512]{1,0:T(8,128)(2,1)S(1)}, bf16[768,512]{1,0:T(8,128)(2,1)}, u32[]{:S(2)}) copy-start(bf16[768,512]{1,0:T(8,128)(2,1)} %vm.3) | copy-start | bytes 2359300
  53.5 3.1 %copy-start.3 = (bf16[768,512]{1,0:T(8,128)(2,1)S(1)}, bf16[768,512]{1,0:T(8,128)(2,1)}, u32[]{:S(2)}) copy-start(bf16[768,512]{1,0:T(8,128)(2,1)} %q.3) | copy-start | bytes 2359300
  78.2 21.8 %copy-start.6 = (bf16[768,768]{0,1:T(8,128)(2,1)S(1)}, bf16[768,768]{0,1:T(8,128)(2,1)}, u32[]{:S(2)}) copy-start(bf16[768,768]{0,1:T(8,128)(2,1)} %copy.11) | copy-start | bytes 3538948
  100.0 75.8 %copy-start.5 = (bf16[768,512]{1,0:T(8,128)(2,1)}, bf16[768,512]{1,0:T(8,128)(2,1)S(1)}, u32[]{:S(2)}) copy-start(bf16[768,512]{1,0:T(8,128)(2,1)S(1)} %constant_dynamic-update-slice_fusion) | copy-start | bytes 2359300
  105.1 44.5 %collective-permute-start.13 = (bf16[4,512,384]{1,2,0:T(8,128)(2,1)S(1)}, bf16[4,512,384]{1,2,0:T(8,128)(2,1)S(1)}, u32[]{:S(2)}, u32[]{:S(2)}) collective-permute-start(bf16[4,512,384]{1,2,0:T(8,128)(2,1)S(1)} %fusion.26), channel_id=1, source_target_pairs={{0,4},{4,0},{8,12},{12,8},{16,20},{20,16},{24,28},{28,24},{1,5},{5... | collective-permute-start | bytes 4718600 | tf_op jit(solution)/shard_map/ppermute | solution.py:150
  107.5 26.6 %collective-permute-start.11 = (bf16[2,768,256]{2,1,0:T(8,128)(2,1)S(1)}, bf16[2,768,256]{2,1,0:T(8,128)(2,1)S(1)}, u32[]{:S(2)}, u32[]{:S(2)}) collective-permute-start(bf16[2,768,256]{2,1,0:T(8,128)(2,1)S(1)} %get-tuple-element.24), channel_id=1, source_target_pairs={{4,12},{8,0},{12,20},{16,8},{20,28},{24,16},{5,13},{9,1},{13,21},{... | collective-permute-start | bytes 2359304 | tf_op jit(solution)/shard_map/ppermute | solution.py:156
  108.8 40.5 %collective-permute-start.9 = (bf16[2,768,256]{2,1,0:T(8,128)(2,1)S(1)}, bf16[2,768,256]{2,1,0:T(8,128)(2,1)S(1)}, u32[]{:S(2)}, u32[]{:S(2)}) collective-permute-start(bf16[2,768,256]{2,1,0:T(8,128)(2,1)S(1)} %get-tuple-element.21), channel_id=1, source_target_pairs={{4,12},{8,0},{12,20},{16,8},{20,28},{24,16},{5,13},{9,1},{13,21},{... | collective-permute-start | bytes 2359304 | tf_op jit(solution)/shard_map/ppermute | solution.py:156
  112.1 63.2 %collective-permute-start.7 = (bf16[2,768,768]{2,1,0:T(8,128)(2,1)S(1)}, bf16[2,768,768]{2,1,0:T(8,128)(2,1)S(1)}, u32[]{:S(2)}, u32[]{:S(2)}) collective-permute-start(bf16[2,768,768]{2,1,0:T(8,128)(2,1)S(1)} %pad_maximum_fusion.1), channel_id=1, source_target_pairs={{0,1},{1,0},{2,3},{3,2},{4,5},{5,4},{6,7},{7,6},{8,9},{9,8},{10,11... | collective-permute-start | bytes 7077896 | tf_op jit(solution)/shard_map/ppermute | solution.py:150
  134.4 25.3 %collective-permute-start.12 = (bf16[2,768,256]{2,1,0:T(8,128)(2,1)S(1)}, bf16[2,768,256]{2,1,0:T(8,128)(2,1)S(1)}, u32[]{:S(2)}, u32[]{:S(2)}) collective-permute-start(bf16[2,768,256]{2,1,0:T(8,128)(2,1)S(1)} %add_convert_fusion.1), channel_id=1, source_target_pairs={{0,4},{4,0},{8,12},{12,8},{16,20},{20,16},{24,28},{28,24},{1,5},{5... | collective-permute-start | bytes 2359304 | tf_op jit(solution)/shard_map/ppermute | solution.py:150
  149.5 25.6 %collective-permute-start.10 = (bf16[2,768,256]{2,1,0:T(8,128)(2,1)S(1)}, bf16[2,768,256]{2,1,0:T(8,128)(2,1)S(1)}, u32[]{:S(2)}, u32[]{:S(2)}) collective-permute-start(bf16[2,768,256]{2,1,0:T(8,128)(2,1)S(1)} %add_convert_fusion.3), channel_id=1, source_target_pairs={{0,4},{4,0},{8,12},{12,8},{16,20},{20,16},{24,28},{28,24},{1,5},{5... | collective-permute-start | bytes 2359304 | tf_op jit(solution)/shard_map/ppermute | solution.py:150
  151.2 28.7 %collective-permute-start.14 = (bf16[2,512,384]{1,2,0:T(8,128)(2,1)S(1)}, bf16[2,512,384]{1,2,0:T(8,128)(2,1)S(1)}, u32[]{:S(2)}, u32[]{:S(2)}) collective-permute-start(bf16[2,512,384]{1,2,0:T(8,128)(2,1)S(1)} %pad_maximum_fusion.7), channel_id=1, source_target_pairs={{0,8},{4,12},{8,0},{12,4},{16,24},{20,28},{24,16},{28,20},{1,9},{5... | collective-permute-start | bytes 2359304 | tf_op jit(solution)/shard_map/ppermute | solution.py:150
  175.8 2.6 %copy-start.4 = (f32[2,768,768]{2,1,0:T(8,128)}, f32[2,768,768]{2,1,0:T(8,128)S(1)}, u32[]{:S(2)}) copy-start(f32[2,768,768]{2,1,0:T(8,128)S(1)} %convert_element_type.70) | copy-start | bytes 14155780
  178.3 28.8 %collective-permute-start.8 = (bf16[768,768]{1,0:T(8,128)(2,1)}, bf16[768,768]{1,0:T(8,128)(2,1)}, u32[]{:S(2)}, u32[]{:S(2)}) collective-permute-start(bf16[768,768]{1,0:T(8,128)(2,1)} %fusion.1), channel_id=1, source_target_pairs={{0,2},{1,3},{2,0},{3,1},{4,6},{5,7},{6,4},{7,5},{8,10},{9,11},{10,... | collective-permute-start | bytes 3538952 | tf_op jit(solution)/shard_map/ppermute | solution.py:150
  180.3 23.5 %collective-permute-start.15 = (bf16[512,384]{0,1:T(8,128)(2,1)S(1)}, bf16[512,384]{0,1:T(8,128)(2,1)S(1)}, u32[]{:S(2)}, u32[]{:S(2)}) collective-permute-start(bf16[512,384]{0,1:T(8,128)(2,1)S(1)} %fusion.49), channel_id=1, source_target_pairs={{0,16},{4,20},{8,24},{12,28},{16,0},{20,4},{24,8},{28,12},{1,17},{... | collective-permute-start | bytes 1179656 | tf_op jit(solution)/shard_map/ppermute | solution.py:150
where the time goes:
time: 214 us; the launch traced here: 211 us
  waiting for transfers between devices  101 us (47%)
  Pallas kernels  43.3 us (20%)
  starting transfers between devices  28.6 us (13%)
  matrix products  19.3 us (9%)
  other arithmetic  10.4 us (5%)
  local copies, waits for them, and re-layouts  8 us (4%)
    ppermute x12, waiting for transfers between devices, swap(): lax.ppermute(x, axis, [(i, i ^ bit) for i in range(lax.axis_size(axis))])  63.9 us
    pallas_call x2, Pallas kernels, attention_call(): pl.pallas_call(functools.partial(attend, rows, tiles), grid_spec=pltpu.Pr...  43.3 us
    ppermute x4, waiting for transfers between devices, shift(): return lax.ppermute(x, axis, [(i, j) for i, j in pairs if 0 <= j < size])  36.7 us
    ppermute x12, starting transfers between devices, swap(): lax.ppermute(x, axis, [(i, i ^ bit) for i in range(lax.axis_size(axis))])  18.5 us
    ppermute x4, starting transfers between devices, shift(): return lax.ppermute(x, axis, [(i, j) for i, j in pairs if 0 <= j < size])  10 us
    dot_general x4, matrix products, dot_nt(): lax.dot_general(a, b, (((1,), (1,)), ((), ())), preferred_element_type=F32)  8.53 us
    dot_general x4, matrix products, dot_nn(): lax.dot_general(a, b, (((1,), (0,)), ((), ())), preferred_element_type=F32)  7.93 us
    unnamed x19, local copies, waits for them, and re-layouts  5.14 us
  transfers between devices with their start and end apart: 16, of which 8 were waited for; matrix products, arithmetic and copies ran while one was open for 12% of the time, Pallas kernels for 10%

commit v1 on v0

--- a/solution.py
+++ b/solution.py
@@ -102,13 +102,14 @@
         rim_near[1] = dv[hi:]
 
 
-def attention_call(place, count, q, g, k, v, far, near, first, heads):
+def attention_call(place, count, q, g, k, v, far, near, first, offset, heads):
     rows = q.shape[0]
     tiles = rows // TILE
     ext = rows + 2 * RIM
     cols = heads * HD
     tile_in = pl.BlockSpec((TILE, HD), lambda h, t, *_: (t, first + h))
     slab_in = pl.BlockSpec((rows, HD), lambda h, t, *_: (0, first + h))
+    rim_in = pl.BlockSpec((2, RIM, HD), lambda h, t, *_: (0, 0, offset + h))
     rim = pl.BlockSpec((2, RIM, HD), lambda h, t, *_: (0, 0, h))
     tile_out = pl.BlockSpec((TILE, HD), lambda h, t, *_: (t, h))
     mid = pl.BlockSpec((2, rows, HD), lambda h, t, *_: (0, 0, h))
@@ -118,7 +119,7 @@
         grid_spec=pltpu.PrefetchScalarGridSpec(
             num_scalar_prefetch=2,
             grid=(heads, tiles),
-            in_specs=[tile_in, tile_in, slab_in, slab_in, rim, rim],
+            in_specs=[tile_in, tile_in, slab_in, slab_in, rim_in, rim_in],
             out_specs=[tile_out, tile_out, mid, rim, rim],
             scratch_shapes=[
                 pltpu.VMEM((ext, HD), BF16),
@@ -144,6 +145,40 @@
             transcendentals=pairs * TILE * TILE,
         ),
     )(place, count, q, g, k, v, far, near)
+
+
+def weight_terms(turned, side, one, two, away_cols, stay_cols, away, stay):
+    a = jnp.concatenate([one[...], two[...]], axis=1)
+    away[0] = dot_tn(a, away_cols[0]).astype(BF16)
+    stay[0] = dot_tn(a, stay_cols[0])
+
+
+def weight_call(turned, side, one, two, stacked, piece):
+    rows = one.shape[0]
+    whole = pl.BlockSpec((rows, HD), lambda k, *_: (0, 0))
+    out = pl.BlockSpec((1, 2 * HD, piece), lambda k, *_: (k, 0, 0))
+    return pl.pallas_call(
+        weight_terms,
+        grid_spec=pltpu.PrefetchScalarGridSpec(
+            num_scalar_prefetch=2,
+            grid=(4,),
+            in_specs=[
+                whole,
+                whole,
+                pl.BlockSpec((1, rows, piece), lambda k, t, x: (t[k], 0, 1 - x[0])),
+                pl.BlockSpec((1, rows, piece), lambda k, t, x: (t[k], 0, x[0])),
+            ],
+            out_specs=[out, out],
+        ),
+        out_shape=[
+            jax.ShapeDtypeStruct((4, 2 * HD, piece), BF16),
+            jax.ShapeDtypeStruct((4, 2 * HD, piece), F32),
+        ],
+        compiler_params=pltpu.CompilerParams(dimension_semantics=("arbitrary",), vmem_limit_bytes=40 << 20),
+        cost_estimate=pl.CostEstimate(
+            flops=2 * rows * 2 * HD * piece * 8, bytes_accessed=rows * piece * 24, transcendentals=0
+        ),
+    )(turned, side, one, two, stacked, stacked)
 
 
 def swap(x, axis, bit):
@@ -170,20 +205,26 @@
     per = heads // chunks
 
     halos = []
+    packs = []
     for n in range(chunks):
         cut = slice(n * per * HD, (n + 1) * per * HD)
-        kv = jnp.stack([key_rows[:, cut], value_rows[:, cut]])
-        near = swap(kv, "seq", 1)
+        packs.append(jnp.stack([key_rows[:, cut], value_rows[:, cut]]))
+    for n in range(chunks):
+        near = swap(packs[n], "seq", 1)
         far = shift(near, "seq", 2)
         halos.append((far, near))
 
     if paired:
-        shards = [cotangent, swap(cotangent, "head", 1), swap(cotangent, "head", 2)]
+        cot, _ = lax.optimization_barrier((cotangent, packs[0]))
+        shards = [cot, swap(cot, "head", 1), swap(cot, "head", 2)]
         shards.append(swap(shards[2], "head", 1))
         weights = [
             lax.dynamic_slice_in_dim(out_weight, (h ^ r) * width, width, 1) for r in range(4)
         ]
         grad_attention = sum(dot_nt(a, b) for a, b in zip(shards, weights)).astype(BF16)
+        stacked = jnp.stack(shards)
+        turned = ((h ^ (s // 2)) ^ jnp.arange(4, dtype=jnp.int32)).astype(jnp.int32)
+        side = (s % 2).astype(jnp.int32).reshape(1)
     else:
         full = lax.all_gather(cotangent, "head", axis=1, tiled=True)
         grad_attention = dot_nt(full, out_weight).astype(BF16)
@@ -193,21 +234,35 @@
     index = jnp.where(alive, neighbours - first, 0)
     span = tiles + REACH
     odd = s % 2 == 1
-    turned = jnp.where(index < REACH, index + span, jnp.where(index >= span, index - span, index))
-    place = jnp.where(odd, turned, index).reshape(-1).astype(jnp.int32)
+    far_first = jnp.where(
+        index < REACH, index + span, jnp.where(index >= span, index - span, index)
+    )
+    place = jnp.where(odd, far_first, index).reshape(-1).astype(jnp.int32)
     count = jnp.sum(alive, axis=1).astype(jnp.int32)
 
-    atts, dqs, dks, dvs, gws = [], [], [], [], []
-    for n in range(chunks):
-        far, near = halos[n]
+    atts, dqs, mids, nears, relays, terms = [], [], [], [], [], []
+    for n in range(heads):
+        far, near = halos[n // per]
+        if n >= 2:
+            place, relays[n - 2] = lax.optimization_barrier((place, relays[n - 2]))
+        if n == 3 and terms:
+            place, away = lax.optimization_barrier((place, terms[0][0]))
+            terms[0] = (away, terms[0][1])
         att, dq, mid, rim_far, rim_near = attention_call(
-            place, count, queries, grad_attention, key_rows, value_rows, far, near, n * per, per
+            place, count, queries, grad_attention, key_rows, value_rows, far, near, n, n % per, 1
         )
-        relayed = shift(rim_far, "seq", -2)
-        back = swap((rim_near + relayed.astype(F32)).astype(BF16), "seq", 1)
-        done = (mid + back.astype(F32)).astype(BF16)
+        relays.append(shift(rim_far, "seq", -2))
         atts.append(att)
         dqs.append(dq)
+        mids.append(mid)
+        nears.append(rim_near)
+        if paired and n % 2 == 1:
+            terms.append(weight_call(turned, side, atts[n - 1], att, stacked, piece))
+
+    dks, dvs = [], []
+    for n in range(heads):
+        back = swap((nears[n] + relays[n].astype(F32)).astype(BF16), "seq", 1)
+        done = (mids[n] + back.astype(F32)).astype(BF16)
         dks.append(done[0])
         dvs.append(done[1])
 
@@ -218,22 +273,13 @@
         got = swap(sent, "head", 1).astype(F32)
         other = swap((parts[2] + got[1]).astype(BF16), "head", 2)
         projected = (parts[0] + got[0] + other.astype(F32)).astype(BF16)
-        stacked = jnp.stack(shards)
-        z, x = s // 2, s % 2
-        turn = h ^ z
-
-        def columns_of(k, side):
-            block = lax.dynamic_index_in_dim(stacked, turn ^ k, 0, False)
-            return lax.dynamic_slice_in_dim(block, side * piece, piece, 1)
-
-        send = jnp.stack([columns_of(k, 1 - x) for k in range(4)])
-        keep = jnp.stack([columns_of(k, x) for k in range(4)])
-        away = jnp.einsum("tc,ktd->kcd", attention, send, preferred_element_type=F32)
-        stay = jnp.einsum("tc,ktd->kcd", attention, keep, preferred_element_type=F32)
-        stay = stay + swap(away.astype(BF16), "seq", 1).astype(F32)
-        got = swap(jnp.stack([stay[1], stay[3]]).astype(BF16), "seq", 2).astype(F32)
-        last = swap((stay[2] + got[1]).astype(BF16), "seq", 4).astype(F32)
-        grad_weight = (stay[0] + got[0] + last) * norm
+        pieces = []
+        for away, stay in terms:
+            stay = stay + swap(away, "seq", 1).astype(F32)
+            got = swap(jnp.stack([stay[1], stay[3]]).astype(BF16), "seq", 2).astype(F32)
+            last = swap((stay[2] + got[1]).astype(BF16), "seq", 4).astype(F32)
+            pieces.append((stay[0] + got[0] + last) * norm)
+        grad_weight = jnp.concatenate(pieces, axis=0)
     else:
         projected = lax.psum_scatter(
             dot_nn(attention, out_weight).astype(BF16), "head", scatter_dimension=1, tiled=True

time: 214 us -> 228 us (1.065)
  Pallas kernels: 43.3 us -> 52.2 us
  starting transfers between devices: 28.6 us -> 37 us
    ppermute x12 -> x17, waiting for transfers between devices: 63.9 us -> 91.9 us  [swap(): lax.ppermute(x, axis, [(i, i ^ bit) for i in range(lax.axis_size(axis))])]
    ppermute x4 -> x6, waiting for transfers between devices: 36.7 us -> 8.67 us  [shift(): return lax.ppermute(x, axis, [(i, j) for i, j in pairs if 0 <= j < size])]
    pallas_call x0 -> x2, Pallas kernels: none -> 7.22 us  [weight_call(): pl.pallas_call(weight_terms, grid_spec=pltpu.PrefetchScalarGridSpec(num_s...]
    ppermute x12 -> x17, starting transfers between devices: 18.5 us -> 24.2 us  [swap(): lax.ppermute(x, axis, [(i, i ^ bit) for i in range(lax.axis_size(axis))])]
    dot_general x2 -> x0, matrix products: 2.85 us -> none  [the longest x1 1.44 us: local(): jnp.einsum('tc,ktd->kcd', attention, keep, preferred_element_type=F32)]
    ppermute x4 -> x6, starting transfers between devices: 10 us -> 12.8 us  [shift(): return lax.ppermute(x, axis, [(i, j) for i, j in pairs if 0 <= j < size])]
    pallas_call x2 -> x4, Pallas kernels: 43.3 us -> 45 us  [attention_call(): pl.pallas_call(functools.partial(attend, rows, tiles), grid_spec=pltpu.Pr...]
    unnamed x19 -> x21, local copies, waits for them, and re-layouts: 5.14 us -> 3.86 us
  transfers between devices with their start and end apart: 16 -> 23, of which waited for: 8 -> 13; matrix products, arithmetic and copies ran while one was open for 12% -> 10% of each run, Pallas kernels for 10% -> 13%
where the time goes in v1:
time: 228 us; the launch traced here: 226 us
  waiting for transfers between devices  101 us (44%)
  Pallas kernels  52.2 us (23%)
  starting transfers between devices  37 us (16%)
  matrix products  17.3 us (8%)
  other arithmetic  11.3 us (5%)
  local copies, waits for them, and re-layouts  6.46 us (3%)
    ppermute x17, waiting for transfers between devices, swap(): lax.ppermute(x, axis, [(i, i ^ bit) for i in range(lax.axis_size(axis))])  91.9 us
    pallas_call x4, Pallas kernels, attention_call(): pl.pallas_call(functools.partial(attend, rows, tiles), grid_spec=pltpu.Pr...  45 us
    ppermute x17, starting transfers between devices, swap(): lax.ppermute(x, axis, [(i, i ^ bit) for i in range(lax.axis_size(axis))])  24.2 us
    ppermute x6, starting transfers between devices, shift(): return lax.ppermute(x, axis, [(i, j) for i, j in pairs if 0 <= j < size])  12.8 us
    dot_general x4, matrix products, dot_nn(): lax.dot_general(a, b, (((1,), (0,)), ((), ())), preferred_element_type=F32)  8.81 us
    ppermute x6, waiting for transfers between devices, shift(): return lax.ppermute(x, axis, [(i, j) for i, j in pairs if 0 <= j < size])  8.67 us
    dot_general x4, matrix products, dot_nt(): lax.dot_general(a, b, (((1,), (1,)), ((), ())), preferred_element_type=F32)  8.51 us
    pallas_call x2, Pallas kernels, weight_call(): pl.pallas_call(weight_terms, grid_spec=pltpu.PrefetchScalarGridSpec(num_s...  7.22 us
  transfers between devices with their start and end apart: 23, of which 13 were waited for; matrix products, arithmetic and copies ran while one was open for 10% of the time, Pallas kernels for 13%

profile of v1, /device:TPU:0, one launch (start us, length us, event | category | flops | bytes accessed | tf_op | source)
XLA Modules:
  0.0 226.0 jit_solution(3116462598849993335)
XLA Ops:
  0.6 1.6 slice_bitcast_fusion.2
  2.3 0.9 pad_maximum_fusion.2
  3.2 3.0 %collective-permute-start.1 = (bf16[768,768]{1,0:T(8,128)(2,1)}, bf16[768,768]{1,0:T(8,128)(2,1)}, u32[]{:S(2)}, u32[]{:S(2)}) collective-permute-start(bf16[768,768]{1,0:T(8,128)(2,1)} %param.10), channel_id=1, source_target_pairs={{0,2},{1,3},{2,0},{3,1},{4,6},{5,7},{6,4},{7,5},{8,10},{9,11},{10,... | collective-permute-start | bytes 3538952 | tf_op jit(solution)/shard_map/ppermute | solution.py:185
  6.2 1.5 collective-permute-start.3
  9.2 23.3 %collective-permute-done.1 = bf16[768,768]{1,0:T(8,128)(2,1)} collective-permute-done((bf16[768,768]{1,0:T(8,128)(2,1)}, bf16[768,768]{1,0:T(8,128)(2,1)}, u32[]{:S(2)}, u32[]{:S(2)}) %collective-permute-start.1) | collective-permute-done | bytes 1179680 | tf_op jit(solution)/shard_map/ppermute | solution.py:185
  32.7 2.1 fusion.16
  34.8 3.8 %collective-permute-start.4 = (bf16[2,768,256]{2,1,0:T(8,128)(2,1)}, bf16[2,768,256]{2,1,0:T(8,128)(2,1)S(1)}, u32[]{:S(2)}, u32[]{:S(2)}) collective-permute-start(bf16[2,768,256]{2,1,0:T(8,128)(2,1)} %collective-permute-done.3.near), channel_id=1, source_target_pairs={{0,8},{8,16},{12,4},{16,24},{20,12},{28,20},{1,9},{9,17},{13,5},{1... | collective-permute-start | bytes 2359304 | tf_op jit(solution)/shard_map/ppermute | solution.py:191
  38.5 3.8 %collective-permute-done.6.near = bf16[2,768,256]{2,1,0:T(8,128)(2,1)} collective-permute-done((bf16[2,768,256]{2,1,0:T(8,128)(2,1)}, bf16[2,768,256]{2,1,0:T(8,128)(2,1)}, u32[]{:S(2)}, u32[]{:S(2)}) %collective-permute-start.6) | collective-permute-done | bytes 786464 | tf_op jit(solution)/shard_map/ppermute | solution.py:185
  42.4 3.5 %collective-permute-start.7 = (bf16[2,768,256]{2,1,0:T(8,128)(2,1)}, bf16[2,768,256]{2,1,0:T(8,128)(2,1)S(1)}, u32[]{:S(2)}, u32[]{:S(2)}) collective-permute-start(bf16[2,768,256]{2,1,0:T(8,128)(2,1)} %collective-permute-done.6.near), channel_id=1, source_target_pairs={{0,8},{8,16},{12,4},{16,24},{20,12},{28,20},{1,9},{9,17},{13,5},{1... | collective-permute-start | bytes 2359304 | tf_op jit(solution)/shard_map/ppermute | solution.py:191
  45.9 2.1 fusion.10
  48.0 2.1 fusion.13
  50.1 2.3 add_convert_fusion.g
  52.4 4.2 %collective-permute-done.4.far = bf16[2,768,256]{2,1,0:T(8,128)(2,1)S(1)} collective-permute-done((bf16[2,768,256]{2,1,0:T(8,128)(2,1)}, bf16[2,768,256]{2,1,0:T(8,128)(2,1)S(1)}, u32[]{:S(2)}, u32[]{:S(2)}) %collective-permute-start.4) | collective-permute-done | bytes 786464 | tf_op jit(solution)/shard_map/ppermute | solution.py:191
  56.6 11.3 %shard_map.102 = (bf16[768,128]{1,0:T(8,128)(2,1)S(1)}, bf16[768,128]{1,0:T(8,128)(2,1)S(1)}, f32[2,768,128]{2,1,0:T(8,128)S(1)}, bf16[2,768,128]{2,1,0:T(8,128)(2,1)S(1)}, f32[2,768,128]{2,1,0:T(8,128)S(1)}) custom-call(s32[8]{0:T(128)S(1)} %reshape.22.place, s32[2]{0:T(128)S(1)} %get-tuple-element.87.count, bf16[768,512]{1,0:T(8,128)(2,1)S(1)} %copy-done.3, ...), custom_call_target="tpu_custom_call" | custom-call | flops 1811939328 | bytes 3932160 | tf_op jit(solution)/shard_map/pallas_call | solution.py:117
  67.9 1.3 collective-permute-start.8
  69.2 11.3 %shard_map.101 = (bf16[768,128]{1,0:T(8,128)(2,1)S(1)}, bf16[768,128]{1,0:T(8,128)(2,1)S(1)}, f32[2,768,128]{2,1,0:T(8,128)S(1)}, bf16[2,768,128]{2,1,0:T(8,128)(2,1)S(1)}, f32[2,768,128]{2,1,0:T(8,128)S(1)}) custom-call(s32[8]{0:T(128)S(1)} %reshape.22.place, s32[2]{0:T(128)S(1)} %get-tuple-element.87.count, bf16[768,512]{1,0:T(8,128)(2,1)S(1)} %copy-done.3, ...), custom_call_target="tpu_custom_call" | custom-call | flops 1811939328 | bytes 3932160 | tf_op jit(solution)/shard_map/pallas_call | solution.py:117
  80.5 1.5 collective-permute-start.5
  82.0 2.6 %pad_maximum_fusion.away_cols.stay_cols = bf16[4,768,768]{2,1,0:T(8,128)(2,1)S(1)} fusion(bf16[1,768,768]{2,1,0:T(8,128)(2,1)} %bitcast.8, bf16[1,768,768]{2,1,0:T(8,128)(2,1)} %bitcast.7, bf16[1,768,768]{2,1,0:T(8,128)(2,1)} %bitcast.6, bf16[1,768,768]{2,1,0:T(8,128)(2,1)} %bitcast.5), kind=kLoop, calls=%fused_computation | loop fusion | flops 7077888 | bytes 9437184 | tf_op jit(solution)/shard_map/stack | solution.py:225
  84.6 3.6 %shard_map.104 = (bf16[4,256,384]{2,1,0:T(8,128)(2,1)S(1)}, f32[4,256,384]{2,1,0:T(8,128)S(1)}) custom-call(s32[4]{0:T(128)S(1)} %iota_xor_fusion.turned, s32[1]{0:T(128)} %bitcast.4.side, bf16[768,128]{1,0:T(8,128)(2,1)S(1)} %get-tuple-element.37.one, bf16[768,128]{1,0:T(8,128)(2,1)S(1)} %get-tuple-element.38.two, ...), custom_call_target="tpu_custom_call" | custom-call | flops 1207959552 | bytes 7077888 | tf_op jit(solution)/shard_map/pallas_call | solution.py:160
  89.8 4.3 %collective-permute-done.5 = bf16[2,768,128]{2,1,0:T(8,128)(2,1)S(1)} collective-permute-done((bf16[2,768,128]{2,1,0:T(8,128)(2,1)S(1)}, bf16[2,768,128]{2,1,0:T(8,128)(2,1)S(1)}, u32[]{:S(2)}, u32[]{:S(2)}) %collective-permute-start.5) | collective-permute-done | bytes 393248 | tf_op jit(solution)/shard_map/ppermute | solution.py:191
  94.0 11.3 %shard_map.103 = (bf16[768,128]{1,0:T(8,128)(2,1)S(1)}, bf16[768,128]{1,0:T(8,128)(2,1)S(1)}, f32[2,768,128]{2,1,0:T(8,128)S(1)}, bf16[2,768,128]{2,1,0:T(8,128)(2,1)S(1)}, f32[2,768,128]{2,1,0:T(8,128)S(1)}) custom-call(s32[8]{0:T(128)S(1)} %reshape.22.place, s32[2]{0:T(128)S(1)} %get-tuple-element.87.count, bf16[768,512]{1,0:T(8,128)(2,1)S(1)} %copy-done.3, ...), custom_call_target="tpu_custom_call" | custom-call | flops 1811939328 | bytes 3932160 | tf_op jit(solution)/shard_map/pallas_call | solution.py:117
  106.0 1.1 copy-done.7
  107.2 11.2 %shard_map.105 = (bf16[768,128]{1,0:T(8,128)(2,1)S(1)}, bf16[768,128]{1,0:T(8,128)(2,1)S(1)}, f32[2,768,128]{2,1,0:T(8,128)S(1)}, bf16[2,768,128]{2,1,0:T(8,128)(2,1)S(1)}, f32[2,768,128]{2,1,0:T(8,128)S(1)}) custom-call(s32[8]{0:T(128)S(1)} %reshape.22.place, s32[2]{0:T(128)S(1)} %get-tuple-element.87.count, bf16[768,512]{1,0:T(8,128)(2,1)S(1)} %copy-done.3, ...), custom_call_target="tpu_custom_call" | custom-call | flops 1811939328 | bytes 3932160 | tf_op jit(solution)/shard_map/pallas_call | solution.py:117
  119.1 1.9 fusion.6
  121.1 1.9 fusion.5
  123.8 2.5 %collective-permute-start.12 = (bf16[2,768,128]{2,1,0:T(8,128)(2,1)}, bf16[2,768,128]{2,1,0:T(8,128)(2,1)S(1)}, u32[]{:S(2)}, u32[]{:S(2)}) collective-permute-start(bf16[2,768,128]{2,1,0:T(8,128)(2,1)} %add_convert_fusion.6), channel_id=1, source_target_pairs={{0,4},{4,0},{8,12},{12,8},{16,20},{20,16},{24,28},{28,24},{1,5},{5... | collective-permute-start | bytes 1179656 | tf_op jit(solution)/shard_map/ppermute | solution.py:185
  126.5 1.3 collective-permute-start.13
  127.8 1.5 collective-permute-start.15
  129.3 3.6 %shard_map.106 = (bf16[4,256,384]{2,1,0:T(8,128)(2,1)S(1)}, f32[4,256,384]{2,1,0:T(8,128)S(1)}) custom-call(s32[4]{0:T(128)S(1)} %iota_xor_fusion.turned, s32[1]{0:T(128)} %bitcast.4.side, bf16[768,128]{1,0:T(8,128)(2,1)S(1)} %get-tuple-element.41.one, bf16[768,128]{1,0:T(8,128)(2,1)S(1)} %get-tuple-element.46.two, ...), custom_call_target="tpu_custom_call" | custom-call | flops 1207959552 | bytes 7077888 | tf_op jit(solution)/shard_map/pallas_call | solution.py:160
  132.9 5.6 %collective-permute-start.20 = (bf16[4,256,384]{2,1,0:T(8,128)(2,1)S(1)}, bf16[4,256,384]{2,1,0:T(8,128)(2,1)S(1)}, u32[]{:S(2)}, u32[]{:S(2)}) collective-permute-start(bf16[4,256,384]{2,1,0:T(8,128)(2,1)S(1)} %get-tuple-element.66), channel_id=1, source_target_pairs={{0,4},{4,0},{8,12},{12,8},{16,20},{20,16},{24,28},{28,24},{1,5},{5... | collective-permute-start | bytes 2359304 | tf_op jit(solution)/shard_map/ppermute | solution.py:185
  138.8 1.0 pad_maximum_fusion.4
  140.6 4.4 %collective-permute-done.11 = bf16[2,768,128]{2,1,0:T(8,128)(2,1)S(1)} collective-permute-done((bf16[2,768,128]{2,1,0:T(8,128)(2,1)S(1)}, bf16[2,768,128]{2,1,0:T(8,128)(2,1)S(1)}, u32[]{:S(2)}, u32[]{:S(2)}) %collective-permute-start.11) | collective-permute-done | bytes 393248 | tf_op jit(solution)/shard_map/ppermute | solution.py:185
  145.0 2.0 collective-permute-start.14
  147.3 14.5 %collective-permute-done.20 = bf16[4,256,384]{2,1,0:T(8,128)(2,1)S(1)} collective-permute-done((bf16[4,256,384]{2,1,0:T(8,128)(2,1)S(1)}, bf16[4,256,384]{2,1,0:T(8,128)(2,1)S(1)}, u32[]{:S(2)}, u32[]{:S(2)}) %collective-permute-start.20) | collective-permute-done | bytes 786464 | tf_op jit(solution)/shard_map/ppermute | solution.py:185
  162.1 2.1 collective-permute-start.21
  164.2 14.4 %collective-permute-done.17 = bf16[4,256,384]{2,1,0:T(8,128)(2,1)S(1)} collective-permute-done((bf16[4,256,384]{2,1,0:T(8,128)(2,1)S(1)}, bf16[4,256,384]{2,1,0:T(8,128)(2,1)S(1)}, u32[]{:S(2)}, u32[]{:S(2)}) %collective-permute-start.17) | collective-permute-done | bytes 786464 | tf_op jit(solution)/shard_map/ppermute | solution.py:185
  179.0 2.1 collective-permute-start.18
  181.1 6.0 %collective-permute-done.14 = bf16[2,768,128]{2,1,0:T(8,128)(2,1)S(1)} collective-permute-done((bf16[2,768,128]{2,1,0:T(8,128)(2,1)S(1)}, bf16[2,768,128]{2,1,0:T(8,128)(2,1)S(1)}, u32[]{:S(2)}, u32[]{:S(2)}) %collective-permute-start.14) | collective-permute-done | bytes 393248 | tf_op jit(solution)/shard_map/ppermute | solution.py:185
  187.2 6.3 %collective-permute-done.16 = bf16[2,768,128]{2,1,0:T(8,128)(2,1)S(1)} collective-permute-done((bf16[2,768,128]{2,1,0:T(8,128)(2,1)S(1)}, bf16[2,768,128]{2,1,0:T(8,128)(2,1)S(1)}, u32[]{:S(2)}, u32[]{:S(2)}) %collective-permute-start.16) | collective-permute-done | bytes 393248 | tf_op jit(solution)/shard_map/ppermute | solution.py:185
  193.7 1.0 pad_maximum_fusion.6
  195.0 1.9 fusion.1
  197.0 1.6 collective-permute-start.10
  198.5 1.0 pad_maximum_fusion.5
  199.6 3.0 %collective-permute-start.22 = (bf16[256,384]{1,0:T(8,128)(2,1)S(1)}, bf16[256,384]{1,0:T(8,128)(2,1)S(1)}, u32[]{:S(2)}, u32[]{:S(2)}) collective-permute-start(bf16[256,384]{1,0:T(8,128)(2,1)S(1)} %fusion.27), channel_id=1, source_target_pairs={{0,16},{4,20},{8,24},{12,28},{16,0},{20,4},{24,8},{28,12},{1,17},{... | collective-permute-start | bytes 589832 | tf_op jit(solution)/shard_map/ppermute | solution.py:185
  202.8 13.2 %collective-permute-done.22 = bf16[256,384]{1,0:T(8,128)(2,1)S(1)} collective-permute-done((bf16[256,384]{1,0:T(8,128)(2,1)S(1)}, bf16[256,384]{1,0:T(8,128)(2,1)S(1)}, u32[]{:S(2)}, u32[]{:S(2)}) %collective-permute-start.22) | collective-permute-done | bytes 196640 | tf_op jit(solution)/shard_map/ppermute | solution.py:185
  216.0 2.0 collective-permute-done.19
  219.0 4.0 %collective-permute-done.10 = bf16[768,768]{1,0:T(8,128)(2,1)S(1)} collective-permute-done((bf16[768,768]{1,0:T(8,128)(2,1)S(1)}, bf16[768,768]{1,0:T(8,128)(2,1)S(1)}, u32[]{:S(2)}, u32[]{:S(2)}) %collective-permute-start.10) | collective-permute-done | bytes 1179680 | tf_op jit(solution)/shard_map/ppermute | solution.py:185
  223.0 3.0 %fusion.4 = bf16[768,768]{1,0:T(8,128)(2,1)} fusion(f32[2,768,768]{2,1,0:T(8,128)S(1)} %convert_element_type.101, bf16[768,768]{1,0:T(8,128)(2,1)S(1)} %collective-permute-done.10, bf16[768,512]{1,0:T(8,128)(2,1)} %constant_dynamic-update-slice_fusion, bf16[512,3072]{1,0:T(8,128)(2,1)S(1)} %copy-done, s32[]{:T(128)S(6)} %select_n.50), kind=kOutput, calls=%fused_computation.7 | convolution fusion | flops 606339072 | bytes 6291460 | tf_op jit(solution)/shard_map/dot_general | solution.py:25
  (71 shorter events, 9.5 us)
Async XLA Ops:
  0.6 32.0 %copy-start = (bf16[512,3072]{1,0:T(8,128)(2,1)S(1)}, bf16[512,3072]{1,0:T(8,128)(2,1)}, u32[]{:S(2)}) copy-start(bf16[512,3072]{1,0:T(8,128)(2,1)} %param.9) | copy-start | bytes 9437188
  2.3 30.2 %copy-start.8 = (s32[2,4]{1,0:T(2,128)S(1)}, s32[2,4]{1,0:T(2,128)}, u32[]{:S(2)}) copy-start(s32[2,4]{1,0:T(2,128)} %param.11) | copy-start | bytes 100
  3.2 29.2 %collective-permute-start.1 = (bf16[768,768]{1,0:T(8,128)(2,1)}, bf16[768,768]{1,0:T(8,128)(2,1)}, u32[]{:S(2)}, u32[]{:S(2)}) collective-permute-start(bf16[768,768]{1,0:T(8,128)(2,1)} %param.10), channel_id=1, source_target_pairs={{0,2},{1,3},{2,0},{3,1},{4,6},{5,7},{6,4},{7,5},{8,10},{9,11},{10,... | collective-permute-start | bytes 3538952 | tf_op jit(solution)/shard_map/ppermute | solution.py:185
  6.2 28.6 %collective-permute-start.3 = (bf16[2,768,256]{2,1,0:T(8,128)(2,1)}, bf16[2,768,256]{2,1,0:T(8,128)(2,1)}, u32[]{:S(2)}, u32[]{:S(2)}) collective-permute-start(bf16[2,768,256]{2,1,0:T(8,128)(2,1)} %pad_maximum_fusion.2), channel_id=1, source_target_pairs={{0,4},{4,0},{8,12},{12,8},{16,20},{20,16},{24,28},{28,24},{1,5},{5... | collective-permute-start | bytes 2359304 | tf_op jit(solution)/shard_map/ppermute | solution.py:185
  7.7 40.3 %collective-permute-start = (bf16[768,768]{1,0:T(8,128)(2,1)}, bf16[768,768]{1,0:T(8,128)(2,1)}, u32[]{:S(2)}, u32[]{:S(2)}) collective-permute-start(bf16[768,768]{1,0:T(8,128)(2,1)} %param.10), channel_id=1, source_target_pairs={{0,1},{1,0},{2,3},{3,2},{4,5},{5,4},{6,7},{7,6},{8,9},{9,8},{10,11... | collective-permute-start | bytes 3538952 | tf_op jit(solution)/shard_map/ppermute | solution.py:185
  8.6 33.7 %collective-permute-start.6 = (bf16[2,768,256]{2,1,0:T(8,128)(2,1)}, bf16[2,768,256]{2,1,0:T(8,128)(2,1)}, u32[]{:S(2)}, u32[]{:S(2)}) collective-permute-start(bf16[2,768,256]{2,1,0:T(8,128)(2,1)} %pad_maximum_fusion.3), channel_id=1, source_target_pairs={{0,4},{4,0},{8,12},{12,8},{16,20},{20,16},{24,28},{28,24},{1,5},{5... | collective-permute-start | bytes 2359304 | tf_op jit(solution)/shard_map/ppermute | solution.py:185
  32.5 17.7 %collective-permute-start.2 = (bf16[768,768]{1,0:T(8,128)(2,1)}, bf16[768,768]{1,0:T(8,128)(2,1)}, u32[]{:S(2)}, u32[]{:S(2)}) collective-permute-start(bf16[768,768]{1,0:T(8,128)(2,1)} %collective-permute-done.1), channel_id=1, source_target_pairs={{0,1},{1,0},{2,3},{3,2},{4,5},{5,4},{6,7},{7,6},{8,9},{9,8},{10,11... | collective-permute-start | bytes 3538952 | tf_op jit(solution)/shard_map/ppermute | solution.py:185
  34.8 21.9 %collective-permute-start.4 = (bf16[2,768,256]{2,1,0:T(8,128)(2,1)}, bf16[2,768,256]{2,1,0:T(8,128)(2,1)S(1)}, u32[]{:S(2)}, u32[]{:S(2)}) collective-permute-start(bf16[2,768,256]{2,1,0:T(8,128)(2,1)} %collective-permute-done.3.near), channel_id=1, source_target_pairs={{0,8},{8,16},{12,4},{16,24},{20,12},{28,20},{1,9},{9,17},{13,5},{1... | collective-permute-start | bytes 2359304 | tf_op jit(solution)/shard_map/ppermute | solution.py:191
  42.4 51.7 %collective-permute-start.7 = (bf16[2,768,256]{2,1,0:T(8,128)(2,1)}, bf16[2,768,256]{2,1,0:T(8,128)(2,1)S(1)}, u32[]{:S(2)}, u32[]{:S(2)}) collective-permute-start(bf16[2,768,256]{2,1,0:T(8,128)(2,1)} %collective-permute-done.6.near), channel_id=1, source_target_pairs={{0,8},{8,16},{12,4},{16,24},{20,12},{28,20},{1,9},{9,17},{13,5},{1... | collective-permute-start | bytes 2359304 | tf_op jit(solution)/shard_map/ppermute | solution.py:191
  50.1 6.5 %copy-start.1 = (bf16[768,512]{1,0:T(8,128)(2,1)S(1)}, bf16[768,512]{1,0:T(8,128)(2,1)}, u32[]{:S(2)}) copy-start(bf16[768,512]{1,0:T(8,128)(2,1)} %km.7) | copy-start | bytes 2359300
  50.1 6.5 %copy-start.2 = (bf16[768,512]{1,0:T(8,128)(2,1)S(1)}, bf16[768,512]{1,0:T(8,128)(2,1)}, u32[]{:S(2)}) copy-start(bf16[768,512]{1,0:T(8,128)(2,1)} %vm.7) | copy-start | bytes 2359300
  50.1 6.5 %copy-start.3 = (bf16[768,512]{1,0:T(8,128)(2,1)S(1)}, bf16[768,512]{1,0:T(8,128)(2,1)}, u32[]{:S(2)}) copy-start(bf16[768,512]{1,0:T(8,128)(2,1)} %q.7) | copy-start | bytes 2359300
  67.9 26.1 %collective-permute-start.8 = (bf16[2,768,128]{2,1,0:T(8,128)(2,1)S(1)}, bf16[2,768,128]{2,1,0:T(8,128)(2,1)S(1)}, u32[]{:S(2)}, u32[]{:S(2)}) collective-permute-start(bf16[2,768,128]{2,1,0:T(8,128)(2,1)S(1)} %get-tuple-element.42), channel_id=1, source_target_pairs={{4,12},{8,0},{12,20},{16,8},{20,28},{24,16},{5,13},{9,1},{13,21},{... | collective-permute-start | bytes 1179656 | tf_op jit(solution)/shard_map/ppermute | solution.py:191
  80.5 13.6 %collective-permute-start.5 = (bf16[2,768,128]{2,1,0:T(8,128)(2,1)S(1)}, bf16[2,768,128]{2,1,0:T(8,128)(2,1)S(1)}, u32[]{:S(2)}, u32[]{:S(2)}) collective-permute-start(bf16[2,768,128]{2,1,0:T(8,128)(2,1)S(1)} %get-tuple-element.39), channel_id=1, source_target_pairs={{4,12},{8,0},{12,20},{16,8},{20,28},{24,16},{5,13},{9,1},{13,21},{... | collective-permute-start | bytes 1179656 | tf_op jit(solution)/shard_map/ppermute | solution.py:191
  88.2 17.1 %copy-start.4 = (bf16[4,256,384]{2,1,0:T(8,128)(2,1)}, bf16[4,256,384]{2,1,0:T(8,128)(2,1)S(1)}, u32[]{:S(2)}) copy-start(bf16[4,256,384]{2,1,0:T(8,128)(2,1)S(1)} %get-tuple-element.64) | copy-start | bytes 2359300
  94.0 11.3 %copy-start.6 = (bf16[2,768,256]{2,1,0:T(8,128)(2,1)}, bf16[2,768,256]{2,1,0:T(8,128)(2,1)S(1)}, u32[]{:S(2)}) copy-start(bf16[2,768,256]{2,1,0:T(8,128)(2,1)S(1)} %collective-permute-done.7.far) | copy-start | bytes 2359300
  106.0 1.1 copy-start.7
  123.8 15.9 %collective-permute-start.12 = (bf16[2,768,128]{2,1,0:T(8,128)(2,1)}, bf16[2,768,128]{2,1,0:T(8,128)(2,1)S(1)}, u32[]{:S(2)}, u32[]{:S(2)}) collective-permute-start(bf16[2,768,128]{2,1,0:T(8,128)(2,1)} %add_convert_fusion.6), channel_id=1, source_target_pairs={{0,4},{4,0},{8,12},{12,8},{16,20},{20,16},{24,28},{28,24},{1,5},{5... | collective-permute-start | bytes 1179656 | tf_op jit(solution)/shard_map/ppermute | solution.py:185
  126.4 18.6 %collective-permute-start.11 = (bf16[2,768,128]{2,1,0:T(8,128)(2,1)S(1)}, bf16[2,768,128]{2,1,0:T(8,128)(2,1)S(1)}, u32[]{:S(2)}, u32[]{:S(2)}) collective-permute-start(bf16[2,768,128]{2,1,0:T(8,128)(2,1)S(1)} %add_convert_fusion.8), channel_id=1, source_target_pairs={{0,4},{4,0},{8,12},{12,8},{16,20},{20,16},{24,28},{28,24},{1,5},{5... | collective-permute-start | bytes 1179656 | tf_op jit(solution)/shard_map/ppermute | solution.py:185
  126.5 14.0 %collective-permute-start.13 = (bf16[2,768,128]{2,1,0:T(8,128)(2,1)S(1)}, bf16[2,768,128]{2,1,0:T(8,128)(2,1)S(1)}, u32[]{:S(2)}, u32[]{:S(2)}) collective-permute-start(bf16[2,768,128]{2,1,0:T(8,128)(2,1)S(1)} %get-tuple-element.59), channel_id=1, source_target_pairs={{4,12},{8,0},{12,20},{16,8},{20,28},{24,16},{5,13},{9,1},{13,21},{... | collective-permute-start | bytes 1179656 | tf_op jit(solution)/shard_map/ppermute | solution.py:191
  127.8 19.4 %collective-permute-start.15 = (bf16[2,768,128]{2,1,0:T(8,128)(2,1)S(1)}, bf16[2,768,128]{2,1,0:T(8,128)(2,1)S(1)}, u32[]{:S(2)}, u32[]{:S(2)}) collective-permute-start(bf16[2,768,128]{2,1,0:T(8,128)(2,1)S(1)} %get-tuple-element.62), channel_id=1, source_target_pairs={{4,12},{8,0},{12,20},{16,8},{20,28},{24,16},{5,13},{9,1},{13,21},{... | collective-permute-start | bytes 1179656 | tf_op jit(solution)/shard_map/ppermute | solution.py:191
  132.9 28.9 %collective-permute-start.20 = (bf16[4,256,384]{2,1,0:T(8,128)(2,1)S(1)}, bf16[4,256,384]{2,1,0:T(8,128)(2,1)S(1)}, u32[]{:S(2)}, u32[]{:S(2)}) collective-permute-start(bf16[4,256,384]{2,1,0:T(8,128)(2,1)S(1)} %get-tuple-element.66), channel_id=1, source_target_pairs={{0,4},{4,0},{8,12},{12,8},{16,20},{20,16},{24,28},{28,24},{1,5},{5... | collective-permute-start | bytes 2359304 | tf_op jit(solution)/shard_map/ppermute | solution.py:185
  138.8 1.4 copy-start.5
  140.2 38.5 %collective-permute-start.17 = (bf16[4,256,384]{2,1,0:T(8,128)(2,1)S(1)}, bf16[4,256,384]{2,1,0:T(8,128)(2,1)S(1)}, u32[]{:S(2)}, u32[]{:S(2)}) collective-permute-start(bf16[4,256,384]{2,1,0:T(8,128)(2,1)S(1)} %copy-done.5), channel_id=1, source_target_pairs={{0,4},{4,0},{8,12},{12,8},{16,20},{20,16},{24,28},{28,24},{1,5},{5... | collective-permute-start | bytes 2359304 | tf_op jit(solution)/shard_map/ppermute | solution.py:185
  140.5 54.2 %collective-permute-start.9 = (bf16[2,768,768]{2,1,0:T(8,128)(2,1)S(1)}, bf16[2,768,768]{2,1,0:T(8,128)(2,1)S(1)}, u32[]{:S(2)}, u32[]{:S(2)}) collective-permute-start(bf16[2,768,768]{2,1,0:T(8,128)(2,1)S(1)} %pad_maximum_fusion.1), channel_id=1, source_target_pairs={{0,1},{1,0},{2,3},{3,2},{4,5},{5,4},{6,7},{7,6},{8,9},{9,8},{10,11... | collective-permute-start | bytes 7077896 | tf_op jit(solution)/shard_map/ppermute | solution.py:185
  145.0 42.1 %collective-permute-start.14 = (bf16[2,768,128]{2,1,0:T(8,128)(2,1)S(1)}, bf16[2,768,128]{2,1,0:T(8,128)(2,1)S(1)}, u32[]{:S(2)}, u32[]{:S(2)}) collective-permute-start(bf16[2,768,128]{2,1,0:T(8,128)(2,1)S(1)} %add_convert_fusion.4), channel_id=1, source_target_pairs={{0,4},{4,0},{8,12},{12,8},{16,20},{20,16},{24,28},{28,24},{1,5},{5... | collective-permute-start | bytes 1179656 | tf_op jit(solution)/shard_map/ppermute | solution.py:185
  147.2 46.3 %collective-permute-start.16 = (bf16[2,768,128]{2,1,0:T(8,128)(2,1)S(1)}, bf16[2,768,128]{2,1,0:T(8,128)(2,1)S(1)}, u32[]{:S(2)}, u32[]{:S(2)}) collective-permute-start(bf16[2,768,128]{2,1,0:T(8,128)(2,1)S(1)} %add_convert_fusion.2), channel_id=1, source_target_pairs={{0,4},{4,0},{8,12},{12,8},{16,20},{20,16},{24,28},{28,24},{1,5},{5... | collective-permute-start | bytes 1179656 | tf_op jit(solution)/shard_map/ppermute | solution.py:185
  162.1 37.4 %collective-permute-start.21 = (bf16[2,256,384]{2,1,0:T(8,128)(2,1)S(1)}, bf16[2,256,384]{2,1,0:T(8,128)(2,1)S(1)}, u32[]{:S(2)}, u32[]{:S(2)}) collective-permute-start(bf16[2,256,384]{2,1,0:T(8,128)(2,1)S(1)} %pad_maximum_fusion.9), channel_id=1, source_target_pairs={{0,8},{4,12},{8,0},{12,4},{16,24},{20,28},{24,16},{28,20},{1,9},{5... | collective-permute-start | bytes 1179656 | tf_op jit(solution)/shard_map/ppermute | solution.py:185
  179.0 23.6 %collective-permute-start.18 = (bf16[2,256,384]{2,1,0:T(8,128)(2,1)S(1)}, bf16[2,256,384]{2,1,0:T(8,128)(2,1)S(1)}, u32[]{:S(2)}, u32[]{:S(2)}) collective-permute-start(bf16[2,256,384]{2,1,0:T(8,128)(2,1)S(1)} %pad_maximum_fusion.8), channel_id=1, source_target_pairs={{0,8},{4,12},{8,0},{12,4},{16,24},{20,28},{24,16},{28,20},{1,9},{5... | collective-permute-start | bytes 1179656 | tf_op jit(solution)/shard_map/ppermute | solution.py:185
  197.0 26.1 %collective-permute-start.10 = (bf16[768,768]{1,0:T(8,128)(2,1)S(1)}, bf16[768,768]{1,0:T(8,128)(2,1)S(1)}, u32[]{:S(2)}, u32[]{:S(2)}) collective-permute-start(bf16[768,768]{1,0:T(8,128)(2,1)S(1)} %fusion.1), channel_id=1, source_target_pairs={{0,2},{1,3},{2,0},{3,1},{4,6},{5,7},{6,4},{7,5},{8,10},{9,11},{10,... | collective-permute-start | bytes 3538952 | tf_op jit(solution)/shard_map/ppermute | solution.py:185
  199.6 16.4 %collective-permute-start.22 = (bf16[256,384]{1,0:T(8,128)(2,1)S(1)}, bf16[256,384]{1,0:T(8,128)(2,1)S(1)}, u32[]{:S(2)}, u32[]{:S(2)}) collective-permute-start(bf16[256,384]{1,0:T(8,128)(2,1)S(1)} %fusion.27), channel_id=1, source_target_pairs={{0,16},{4,20},{8,24},{12,28},{16,0},{20,4},{24,8},{28,12},{1,17},{... | collective-permute-start | bytes 589832 | tf_op jit(solution)/shard_map/ppermute | solution.py:185
  202.7 15.4 %collective-permute-start.19 = (bf16[256,384]{1,0:T(8,128)(2,1)S(1)}, bf16[256,384]{1,0:T(8,128)(2,1)S(1)}, u32[]{:S(2)}, u32[]{:S(2)}) collective-permute-start(bf16[256,384]{1,0:T(8,128)(2,1)S(1)} %fusion.26), channel_id=1, source_target_pairs={{0,16},{4,20},{8,24},{12,28},{16,0},{20,4},{24,8},{28,12},{1,17},{... | collective-permute-start | bytes 589832 | tf_op jit(solution)/shard_map/ppermute | solution.py:185

commit v2 on v0

--- a/solution.py
+++ b/solution.py
@@ -156,6 +156,215 @@
     return lax.ppermute(x, axis, [(i, j) for i, j in pairs if 0 <= j < size])
 
 
+MESH = pl.DeviceIdType.MESH
+
+
+def finish(
+    chunks, seq, norm,
+    att, stacked, weight, rim_far, rim_near, mid,
+    projected, dkv, grad_weight,
+    far_in, near_out, near_in, gw_out, gw_in, gw_sum, two_out, two_in, four_out, four_in,
+    core_out, core_in, mine, theirs, y_out, y_in,
+    far_s, far_r, near_s, near_r, gw_s, gw_r, two_s, two_r, four_s, four_r, core_s, core_r, y_s, y_r,
+):
+    s, h = lax.axis_index("seq"), lax.axis_index("head")
+    x, z0, z1 = s % 2, (s // 2) % 2, (s // 4) % 2
+    h0, h1 = h % 2, (h // 2) % 2
+    beside = (s + 1 - 2 * x, h)
+    hop2 = (s + 2 - 4 * z0, h)
+    hop4 = (s + 4 - 8 * z1, h)
+    mate = (s, h + 1 - 2 * h0)
+    across = (s, h + 2 - 4 * h1)
+    below, above = s >= 2, s + 2 < seq
+    width = projected.shape[1]
+    piece = grad_weight.shape[1]
+    part = att[0].shape[1]
+
+    def send(src, dst, sems, semr, i, dev):
+        return pltpu.make_async_remote_copy(
+            src_ref=src, dst_ref=dst, send_sem=sems.at[i], recv_sem=semr.at[i],
+            device_id=dev, device_id_type=MESH,
+        )
+
+    barrier = pltpu.get_barrier_semaphore()
+    for dev in (beside, hop4, mate, across):
+        pl.semaphore_signal(barrier, inc=1, device_id=dev, device_id_type=MESH)
+
+    @pl.when(below)
+    def _():
+        pl.semaphore_signal(barrier, inc=1, device_id=(s - 2, h), device_id_type=MESH)
+
+    @pl.when(above)
+    def _():
+        pl.semaphore_signal(barrier, inc=1, device_id=(s + 2, h), device_id_type=MESH)
+
+    pl.semaphore_wait(barrier, 4 + (s + seq - 2) // seq + (2 * seq - 3 - s) // seq)
+
+    down = s - 2 + 4 * x
+    sends_far = (down >= 0) & (down < seq)
+    up = s + 2 - 4 * x
+    gets_far = (up >= 0) & (up < seq)
+    fars = [send(rim_far[c], far_in.at[c], far_s, far_r, c, (down, h)) for c in range(chunks)]
+
+    @pl.when(sends_far)
+    def _():
+        for copy in fars:
+            copy.start()
+
+    def columns(k, side):
+        r = (h0 + z0 + k % 2) % 2 + 2 * ((h1 + z1 + k // 2) % 2)
+        return stacked[r, :, pl.ds(pl.multiple_of(side * piece, piece), piece)]
+
+    gws = []
+    for k in (1, 3, 2, 0):
+        cot = columns(k, 1 - x)
+        for c in range(chunks):
+            gw_out[k, c * part : (c + 1) * part] = dot_tn(att[c][...], cot).astype(BF16)
+        gws.append(send(gw_out.at[k], gw_in.at[k], gw_s, gw_r, k, beside))
+        gws[-1].start()
+
+    def share(r):
+        b0, b1 = (h0 + r % 2) % 2, (h1 + r // 2) % 2
+        at = pl.ds(pl.multiple_of((b0 + 2 * b1) * width, width), width)
+        total = dot_nn(att[0][...], weight[:part, at])
+        for c in range(1, chunks):
+            total += dot_nn(att[c][...], weight[c * part : (c + 1) * part, at])
+        return total
+
+    cores = []
+    for i, r in enumerate((3, 1)):
+        core_out[i] = share(r).astype(BF16)
+        cores.append(send(core_out.at[i], core_in.at[i], core_s, core_r, i, mate))
+        cores[-1].start()
+    theirs[...] = share(2)
+    cores[0].wait_recv()
+    y_out[...] = (theirs[...] + core_in[0].astype(F32)).astype(BF16)
+    ys = send(y_out, y_in, y_s, y_r, 0, across)
+    ys.start()
+
+    nears = []
+    for c in range(chunks):
+        nears.append(send(near_out.at[c], near_in.at[c], near_s, near_r, c, beside))
+
+        @pl.when(gets_far)
+        def _():
+            fars[c].wait_recv()
+            for i in range(2):
+                near_out[c, i] = (rim_near[c][i] + far_in[c, i].astype(F32)).astype(BF16)
+
+        @pl.when(jnp.logical_not(gets_far))
+        def _():
+            for i in range(2):
+                near_out[c, i] = rim_near[c][i].astype(BF16)
+
+        nears[c].start()
+
+    for k in range(4):
+        cot = columns(k, x)
+        for c in range(chunks):
+            gw_sum[k, c * part : (c + 1) * part] = dot_tn(att[c][...], cot)
+    mine[...] = share(0)
+    cores[1].wait_recv()
+    mine[...] += core_in[1].astype(F32)
+
+    twos = []
+    for i, k in enumerate((1, 3)):
+        gws[i].wait_recv()
+        two_out[i] = (gw_sum[k] + gw_in[k].astype(F32)).astype(BF16)
+        twos.append(send(two_out.at[i], two_in.at[i], two_s, two_r, i, hop2))
+    twos[1].start()
+    twos[0].start()
+    gws[2].wait_recv()
+    gw_sum[2] += gw_in[2].astype(F32)
+    gws[3].wait_recv()
+    gw_sum[0] += gw_in[0].astype(F32)
+    twos[1].wait_recv()
+    four_out[...] = (gw_sum[2] + two_in[1].astype(F32)).astype(BF16)
+    four = send(four_out, four_in, four_s, four_r, 0, hop4)
+    four.start()
+    twos[0].wait_recv()
+    gw_sum[0] += two_in[0].astype(F32)
+
+    ys.wait_recv()
+    projected[...] = (mine[...] + y_in[...].astype(F32)).astype(BF16)
+    four.wait_recv()
+    grad_weight[...] = (gw_sum[0] + four_in[...].astype(F32)) * norm
+    for c in range(chunks):
+        nears[c].wait_recv()
+        for i in range(2):
+            dkv[i, :, c * part : (c + 1) * part] = (mid[c][i] + near_in[c, i].astype(F32)).astype(BF16)
+
+    @pl.when(sends_far)
+    def _():
+        for copy in fars:
+            copy.wait_send()
+
+    for copy in gws + cores + nears + twos + [ys, four]:
+        copy.wait_send()
+
+
+def finish_call(atts, stacked, weight, fars, nears, mids, seq, norm):
+    chunks = len(atts)
+    rows, part = atts[0].shape
+    depth = chunks * part
+    width = stacked.shape[2]
+    piece = width * 4 // seq
+    vmem = pl.BlockSpec(memory_space=pltpu.VMEM)
+    rim = (chunks, 2, RIM, part)
+    sem = pltpu.SemaphoreType.DMA
+
+    def kernel(*refs):
+        refs = list(refs)
+
+        def take(n):
+            got = refs[:n]
+            del refs[:n]
+            return got
+
+        att = take(chunks)
+        stack_ref, weight_ref = take(2)
+        far, near, mid = take(chunks), take(chunks), take(chunks)
+        finish(chunks, seq, norm, att, stack_ref, weight_ref, far, near, mid, *refs)
+
+    return pl.pallas_call(
+        kernel,
+        in_specs=[vmem] * (4 * chunks + 2),
+        out_specs=[vmem] * 3,
+        out_shape=[
+            jax.ShapeDtypeStruct((rows, width), BF16),
+            jax.ShapeDtypeStruct((2, rows, depth), BF16),
+            jax.ShapeDtypeStruct((depth, piece), F32),
+        ],
+        scratch_shapes=[
+            pltpu.VMEM(rim, BF16),
+            pltpu.VMEM(rim, BF16),
+            pltpu.VMEM(rim, BF16),
+            pltpu.VMEM((4, depth, piece), BF16),
+            pltpu.VMEM((4, depth, piece), BF16),
+            pltpu.VMEM((4, depth, piece), F32),
+            pltpu.VMEM((2, depth, piece), BF16),
+            pltpu.VMEM((2, depth, piece), BF16),
+            pltpu.VMEM((depth, piece), BF16),
+            pltpu.VMEM((depth, piece), BF16),
+            pltpu.VMEM((2, rows, width), BF16),
+            pltpu.VMEM((2, rows, width), BF16),
+            pltpu.VMEM((rows, width), F32),
+            pltpu.VMEM((rows, width), F32),
+            pltpu.VMEM((rows, width), BF16),
+            pltpu.VMEM((rows, width), BF16),
+            sem((chunks,)), sem((chunks,)), sem((chunks,)), sem((chunks,)),
+            sem((4,)), sem((4,)), sem((2,)), sem((2,)), sem((1,)), sem((1,)),
+            sem((2,)), sem((2,)), sem((1,)), sem((1,)),
+        ],
+        compiler_params=pltpu.CompilerParams(
+            collective_id=0, has_side_effects=True, vmem_limit_bytes=60 << 20
+        ),
+        cost_estimate=pl.CostEstimate(
+            flops=4 * rows * depth * width * 4, bytes_accessed=40 << 20, transcendentals=0
+        ),
+    )(*atts, stacked, weight, *fars, *nears, *mids)
+
+
 def local(queries, key_rows, value_rows, out_weight, cotangent, neighbours):
     rows, columns = queries.shape
     heads = columns // HD
@@ -197,56 +406,45 @@
     place = jnp.where(odd, turned, index).reshape(-1).astype(jnp.int32)
     count = jnp.sum(alive, axis=1).astype(jnp.int32)
 
-    atts, dqs, dks, dvs, gws = [], [], [], [], []
+    atts, dqs, mids, fars, nears = [], [], [], [], []
     for n in range(chunks):
         far, near = halos[n]
         att, dq, mid, rim_far, rim_near = attention_call(
             place, count, queries, grad_attention, key_rows, value_rows, far, near, n * per, per
         )
-        relayed = shift(rim_far, "seq", -2)
-        back = swap((rim_near + relayed.astype(F32)).astype(BF16), "seq", 1)
-        done = (mid + back.astype(F32)).astype(BF16)
         atts.append(att)
         dqs.append(dq)
+        mids.append(mid)
+        fars.append(rim_far)
+        nears.append(rim_near)
+
+    grad_queries = jnp.concatenate(dqs, axis=1)
+    if paired:
+        projected, dkv, grad_weight = finish_call(
+            atts, jnp.stack(shards), out_weight, fars, nears, mids, seq, norm
+        )
+        return (projected, grad_queries, dkv[0], dkv[1], grad_weight)
+
+    dks, dvs = [], []
+    for n in range(chunks):
+        relayed = shift(fars[n], "seq", -2)
+        back = swap((nears[n] + relayed.astype(F32)).astype(BF16), "seq", 1)
+        done = (mids[n] + back.astype(F32)).astype(BF16)
         dks.append(done[0])
         dvs.append(done[1])
-
     attention = jnp.concatenate(atts, axis=1)
-    if paired:
-        parts = [dot_nn(attention, w) for w in weights]
-        sent = jnp.stack([parts[1], parts[3]]).astype(BF16)
-        got = swap(sent, "head", 1).astype(F32)
-        other = swap((parts[2] + got[1]).astype(BF16), "head", 2)
-        projected = (parts[0] + got[0] + other.astype(F32)).astype(BF16)
-        stacked = jnp.stack(shards)
-        z, x = s // 2, s % 2
-        turn = h ^ z
-
-        def columns_of(k, side):
-            block = lax.dynamic_index_in_dim(stacked, turn ^ k, 0, False)
-            return lax.dynamic_slice_in_dim(block, side * piece, piece, 1)
-
-        send = jnp.stack([columns_of(k, 1 - x) for k in range(4)])
-        keep = jnp.stack([columns_of(k, x) for k in range(4)])
-        away = jnp.einsum("tc,ktd->kcd", attention, send, preferred_element_type=F32)
-        stay = jnp.einsum("tc,ktd->kcd", attention, keep, preferred_element_type=F32)
-        stay = stay + swap(away.astype(BF16), "seq", 1).astype(F32)
-        got = swap(jnp.stack([stay[1], stay[3]]).astype(BF16), "seq", 2).astype(F32)
-        last = swap((stay[2] + got[1]).astype(BF16), "seq", 4).astype(F32)
-        grad_weight = (stay[0] + got[0] + last) * norm
-    else:
-        projected = lax.psum_scatter(
-            dot_nn(attention, out_weight).astype(BF16), "head", scatter_dimension=1, tiled=True
-        )
-        grad_weight = (
-            lax.psum_scatter(
-                dot_tn(attention, full).astype(BF16), "seq", scatter_dimension=1, tiled=True
-            ).astype(F32)
-            * norm
-        )
+    projected = lax.psum_scatter(
+        dot_nn(attention, out_weight).astype(BF16), "head", scatter_dimension=1, tiled=True
+    )
+    grad_weight = (
+        lax.psum_scatter(
+            dot_tn(attention, full).astype(BF16), "seq", scatter_dimension=1, tiled=True
+        ).astype(F32)
+        * norm
+    )
     return (
         projected,
-        jnp.concatenate(dqs, axis=1),
+        grad_queries,
         jnp.concatenate(dks, axis=1),
         jnp.concatenate(dvs, axis=1),
         grad_weight,

time: 214 us -> 214 us (level); the launches traced: 211 us -> 213 us
  Pallas kernels: 43.3 us -> 128 us
  waiting for transfers between devices: 101 us -> 47.3 us
  starting transfers between devices: 28.6 us -> 12.4 us
  matrix products: 19.3 us -> 7.47 us
  other arithmetic: 10.4 us -> 6.91 us
  local copies, waits for them, and re-layouts: 8 us -> 10.7 us
    pallas_call x0 -> x1, Pallas kernels: none -> 90.7 us  [finish_call(): pl.pallas_call(kernel, in_specs=[vmem] * (4 * chunks + 2), out_specs=[vme...]
    ppermute x12 -> x5, waiting for transfers between devices: 63.9 us -> 27.4 us  [swap(): lax.ppermute(x, axis, [(i, i ^ bit) for i in range(lax.axis_size(axis))])]
    ppermute x4 -> x2, waiting for transfers between devices: 36.7 us -> 19.9 us  [shift(): return lax.ppermute(x, axis, [(i, j) for i, j in pairs if 0 <= j < size])]
    ppermute x12 -> x5, starting transfers between devices: 18.5 us -> 5.13 us  [swap(): lax.ppermute(x, axis, [(i, i ^ bit) for i in range(lax.axis_size(axis))])]
    dot_general x6 -> x0, matrix products: 10.8 us -> none  [the longest x4 7.93 us: dot_nn(): lax.dot_general(a, b, (((1,), (0,)), ((), ())), preferred_element_type=F32)]
    pallas_call x2, Pallas kernels: 43.3 us -> 37 us  [attention_call(): pl.pallas_call(functools.partial(attend, rows, tiles), grid_spec=pltpu.Pr...]
    ppermute x4 -> x2, starting transfers between devices: 10 us -> 7.27 us  [shift(): return lax.ppermute(x, axis, [(i, j) for i, j in pairs if 0 <= j < size])]
    squeeze x2 -> x1, local copies, waits for them, and re-layouts: 0.1 us -> 2.61 us  [local(): return (projected, grad_queries, dkv[0], dkv[1], grad_weight)]
  transfers between devices with their start and end apart: 16 -> 7, of which waited for: 8 -> 3; matrix products, arithmetic and copies ran while one was open for 12% -> 7% of each run, Pallas kernels for 10% -> 9%
where the time goes in v2:
time: 214 us; the launch traced here: 213 us
  Pallas kernels  128 us (60%)
  waiting for transfers between devices  47.3 us (22%)
  starting transfers between devices  12.4 us (6%)
  local copies, waits for them, and re-layouts  10.7 us (5%)
  matrix products  7.47 us (3%)
  other arithmetic  6.91 us (3%)
    pallas_call x1, Pallas kernels, finish_call(): pl.pallas_call(kernel, in_specs=[vmem] * (4 * chunks + 2), out_specs=[vme...  90.7 us
    pallas_call x2, Pallas kernels, attention_call(): pl.pallas_call(functools.partial(attend, rows, tiles), grid_spec=pltpu.Pr...  37 us
    ppermute x5, waiting for transfers between devices, swap(): lax.ppermute(x, axis, [(i, i ^ bit) for i in range(lax.axis_size(axis))])  27.4 us
    ppermute x2, waiting for transfers between devices, shift(): return lax.ppermute(x, axis, [(i, j) for i, j in pairs if 0 <= j < size])  19.9 us
    dot_general x4, matrix products, dot_nt(): lax.dot_general(a, b, (((1,), (1,)), ((), ())), preferred_element_type=F32)  7.47 us
    ppermute x2, starting transfers between devices, shift(): return lax.ppermute(x, axis, [(i, j) for i, j in pairs if 0 <= j < size])  7.27 us
    unnamed x34, local copies, waits for them, and re-layouts  6.59 us
    ppermute x5, starting transfers between devices, swap(): lax.ppermute(x, axis, [(i, i ^ bit) for i in range(lax.axis_size(axis))])  5.13 us
  transfers between devices with their start and end apart: 7, of which 3 were waited for; matrix products, arithmetic and copies ran while one was open for 7% of the time, Pallas kernels for 9%

profile of v2, /device:TPU:0, one launch (start us, length us, event | category | flops | bytes accessed | tf_op | source)
XLA Modules:
  0.0 213.4 jit_solution(1390523360319041392)
XLA Ops:
  0.6 3.0 %collective-permute-start.1 = (bf16[768,768]{1,0:T(8,128)(2,1)}, bf16[768,768]{1,0:T(8,128)(2,1)}, u32[]{:S(2)}, u32[]{:S(2)}) collective-permute-start(bf16[768,768]{1,0:T(8,128)(2,1)} %param.10), channel_id=1, source_target_pairs={{0,2},{1,3},{2,0},{3,1},{4,6},{5,7},{6,4},{7,5},{8,10},{9,11},{10,... | collective-permute-start | bytes 3538952 | tf_op jit(solution)/shard_map/ppermute | solution.py:150
  3.7 0.0 collective-permute-start
  3.7 1.5 slice_bitcast_fusion.2
  5.1 0.0 copy-start.15
  5.1 0.1 pad_maximum_fusion.1
  5.2 1.6 collective-permute-start.3
  6.8 0.9 pad_maximum_fusion.2
  7.7 0.5 collective-permute-start.5
  8.3 21.7 %collective-permute-done.1 = bf16[768,768]{1,0:T(8,128)(2,1)} collective-permute-done((bf16[768,768]{1,0:T(8,128)(2,1)}, bf16[768,768]{1,0:T(8,128)(2,1)}, u32[]{:S(2)}, u32[]{:S(2)}) %collective-permute-start.1) | collective-permute-done | bytes 1179680 | tf_op jit(solution)/shard_map/ppermute | solution.py:150
  29.9 0.0 collective-permute-start.2
  30.0 0.0 copy-done.15
  30.0 0.1 convert_reduce_fusion
  30.1 0.1 reshape.13.place
  30.2 2.5 %fusion.6 = f32[512,768]{0,1:T(8,128)S(1)} fusion(bf16[768,768]{1,0:T(8,128)(2,1)} %param.10, bf16[512,3072]{1,0:T(8,128)(2,1)} %refs_3_.1, s32[]{:T(128)S(6)} %select_n.44), kind=kOutput, calls=%fused_computation.13 | convolution fusion | flops 603979776 | bytes 3538948 | tf_op jit(solution)/shard_map/dot_general | solution.py:21
  32.6 0.0 collective-permute-done.3.near
  32.6 3.7 %collective-permute-start.4 = (bf16[2,768,256]{2,1,0:T(8,128)(2,1)S(1)}, bf16[2,768,256]{2,1,0:T(8,128)(2,1)S(1)}, u32[]{:S(2)}, u32[]{:S(2)}) collective-permute-start(bf16[2,768,256]{2,1,0:T(8,128)(2,1)S(1)} %collective-permute-done.3.near), channel_id=1, source_target_pairs={{0,8},{8,16},{12,4},{16,24},{20,12},{28,20},{1,9},{9,17},{13,5},{1... | collective-permute-start | bytes 2359304 | tf_op jit(solution)/shard_map/ppermute | solution.py:156
  36.4 5.7 %collective-permute-done.5.near = bf16[2,768,256]{2,1,0:T(8,128)(2,1)S(1)} collective-permute-done((bf16[2,768,256]{2,1,0:T(8,128)(2,1)}, bf16[2,768,256]{2,1,0:T(8,128)(2,1)S(1)}, u32[]{:S(2)}, u32[]{:S(2)}) %collective-permute-start.5) | collective-permute-done | bytes 786464 | tf_op jit(solution)/shard_map/ppermute | solution.py:150
  42.1 3.5 %collective-permute-start.6 = (bf16[2,768,256]{2,1,0:T(8,128)(2,1)S(1)}, bf16[2,768,256]{2,1,0:T(8,128)(2,1)S(1)}, u32[]{:S(2)}, u32[]{:S(2)}) collective-permute-start(bf16[2,768,256]{2,1,0:T(8,128)(2,1)S(1)} %collective-permute-done.5.near), channel_id=1, source_target_pairs={{0,8},{8,16},{12,4},{16,24},{20,12},{28,20},{1,9},{9,17},{13,5},{1... | collective-permute-start | bytes 2359304 | tf_op jit(solution)/shard_map/ppermute | solution.py:156
  45.6 0.0 copy-done.14
  45.6 2.1 fusion.2
  47.7 0.0 collective-permute-done
  47.7 2.1 fusion.4
  49.8 0.0 copy-start
  49.8 0.0 copy-start.1
  49.9 0.0 copy-start.2
  49.9 0.0 collective-permute-done.2
  49.9 0.8 fusion.g
  50.7 19.9 %collective-permute-done.6.far = bf16[2,768,256]{2,1,0:T(8,128)(2,1)S(1)} collective-permute-done((bf16[2,768,256]{2,1,0:T(8,128)(2,1)S(1)}, bf16[2,768,256]{2,1,0:T(8,128)(2,1)S(1)}, u32[]{:S(2)}, u32[]{:S(2)}) %collective-permute-start.6) | collective-permute-done | bytes 786464 | tf_op jit(solution)/shard_map/ppermute | solution.py:156
  70.6 0.0 copy-done
  70.7 0.0 copy-done.1
  70.7 0.0 copy-done.2
  70.7 18.6 %shard_map.102 = (bf16[768,256]{1,0:T(8,128)(2,1)S(1)}, bf16[768,256]{1,0:T(8,128)(2,1)S(1)}, f32[2,768,256]{2,1,0:T(8,128)S(1)}, bf16[2,768,256]{2,1,0:T(8,128)(2,1)S(1)}, f32[2,768,256]{2,1,0:T(8,128)S(1)}) custom-call(s32[8]{0:T(128)S(1)} %reshape.13.place, s32[2]{0:T(128)S(1)} %get-tuple-element.37.count, bf16[768,512]{1,0:T(8,128)(2,1)S(1)} %copy-done.2, ...), custom_call_target="tpu_custom_call" | custom-call | flops 3623878656 | bytes 7864320 | tf_op jit(solution)/shard_map/pallas_call | solution.py:116
  89.3 0.0 copy-start.7
  89.3 0.0 copy-start.9
  89.3 4.8 %pad_maximum_fusion.refs_2_ = bf16[4,768,768]{2,1,0:T(8,128)(2,1)} fusion(bf16[1,768,768]{2,1,0:T(8,128)(2,1)S(1)} %bitcast.22, bf16[1,768,768]{2,1,0:T(8,128)(2,1)} %bitcast.7, bf16[1,768,768]{2,1,0:T(8,128)(2,1)} %bitcast.6, bf16[1,768,768]{2,1,0:T(8,128)(2,1)S(1)} %bitcast.23), kind=kLoop, calls=%fused_computation | loop fusion | flops 7077888 | bytes 9437184 | tf_op jit(solution)/shard_map/stack | solution.py:424
  94.1 0.0 copy-done.4
  94.2 0.0 collective-permute-done.4.far
  94.2 18.4 %shard_map.101 = (bf16[768,256]{1,0:T(8,128)(2,1)S(1)}, bf16[768,256]{1,0:T(8,128)(2,1)S(1)}, f32[2,768,256]{2,1,0:T(8,128)S(1)}, bf16[2,768,256]{2,1,0:T(8,128)(2,1)S(1)}, f32[2,768,256]{2,1,0:T(8,128)S(1)}) custom-call(s32[8]{0:T(128)S(1)} %reshape.13.place, s32[2]{0:T(128)S(1)} %get-tuple-element.37.count, bf16[768,512]{1,0:T(8,128)(2,1)S(1)} %copy-done.2, ...), custom_call_target="tpu_custom_call" | custom-call | flops 3623878656 | bytes 7864320 | tf_op jit(solution)/shard_map/pallas_call | solution.py:116
  112.6 1.1 copy-done.5
  113.8 1.3 copy-done.6
  115.0 0.9 copy-done.8
  115.9 0.7 copy-done.10
  116.6 90.7 %shard_map.103 = (bf16[768,768]{1,0:T(8,128)(2,1)}, bf16[2,768,512]{2,1,0:T(8,128)(2,1)}, f32[512,384]{1,0:T(8,128)}) custom-call(bf16[768,256]{1,0:T(8,128)(2,1)} %copy-done.10, bf16[768,256]{1,0:T(8,128)(2,1)} %copy-done.9, bf16[4,768,768]{2,1,0:T(8,128)(2,1)} %pad_maximum_fusion.refs_2_, bf16[512,3072]{1,0:T(8,128)(2,1)} %refs_3_.1, ...), custom_call_target="tpu_custom_call" | custom-call | flops 4831838208 | bytes 41943040 | tf_op jit(solution)/shard_map/pallas_call | solution.py:329
  207.4 2.6 %slice_bitcast_fusion = (bf16[768,512]{1,0:T(8,128)(2,1)}, bf16[768,512]{1,0:T(8,128)(2,1)}) fusion(bf16[2,768,512]{2,1,0:T(8,128)(2,1)} %get-tuple-element.29), kind=kLoop, calls=%fused_computation.6 | loop fusion | bytes 3145728 | tf_op jit(solution)/shard_map/squeeze | solution.py:426
  210.0 0.9 pad_maximum_fusion.3
  210.9 0.6 copy-done.12
  211.5 1.0 copy.21
  212.6 0.9 copy.22
  (15 shorter events, 0.0 us)
Async XLA Ops:
  0.6 29.3 %collective-permute-start.1 = (bf16[768,768]{1,0:T(8,128)(2,1)}, bf16[768,768]{1,0:T(8,128)(2,1)}, u32[]{:S(2)}, u32[]{:S(2)}) collective-permute-start(bf16[768,768]{1,0:T(8,128)(2,1)} %param.10), channel_id=1, source_target_pairs={{0,2},{1,3},{2,0},{3,1},{4,6},{5,7},{6,4},{7,5},{8,10},{9,11},{10,... | collective-permute-start | bytes 3538952 | tf_op jit(solution)/shard_map/ppermute | solution.py:150
  3.7 44.1 %collective-permute-start = (bf16[768,768]{1,0:T(8,128)(2,1)}, bf16[768,768]{1,0:T(8,128)(2,1)}, u32[]{:S(2)}, u32[]{:S(2)}) collective-permute-start(bf16[768,768]{1,0:T(8,128)(2,1)} %param.10), channel_id=1, source_target_pairs={{0,1},{1,0},{2,3},{3,2},{4,5},{5,4},{6,7},{7,6},{8,9},{9,8},{10,11... | collective-permute-start | bytes 3538952 | tf_op jit(solution)/shard_map/ppermute | solution.py:150
  5.1 24.8 %copy-start.15 = (s32[2,4]{1,0:T(2,128)S(1)}, s32[2,4]{1,0:T(2,128)}, u32[]{:S(2)}) copy-start(s32[2,4]{1,0:T(2,128)} %param.11) | copy-start | bytes 100
  5.2 27.4 %collective-permute-start.3 = (bf16[2,768,256]{2,1,0:T(8,128)(2,1)S(1)}, bf16[2,768,256]{2,1,0:T(8,128)(2,1)S(1)}, u32[]{:S(2)}, u32[]{:S(2)}) collective-permute-start(bf16[2,768,256]{2,1,0:T(8,128)(2,1)S(1)} %pad_maximum_fusion.1), channel_id=1, source_target_pairs={{0,4},{4,0},{8,12},{12,8},{16,20},{20,16},{24,28},{28,24},{1,5},{5... | collective-permute-start | bytes 2359304 | tf_op jit(solution)/shard_map/ppermute | solution.py:150
  7.7 34.4 %collective-permute-start.5 = (bf16[2,768,256]{2,1,0:T(8,128)(2,1)}, bf16[2,768,256]{2,1,0:T(8,128)(2,1)S(1)}, u32[]{:S(2)}, u32[]{:S(2)}) collective-permute-start(bf16[2,768,256]{2,1,0:T(8,128)(2,1)} %pad_maximum_fusion.2), channel_id=1, source_target_pairs={{0,4},{4,0},{8,12},{12,8},{16,20},{20,16},{24,28},{28,24},{1,5},{5... | collective-permute-start | bytes 2359304 | tf_op jit(solution)/shard_map/ppermute | solution.py:150
  29.9 19.9 %collective-permute-start.2 = (bf16[768,768]{1,0:T(8,128)(2,1)}, bf16[768,768]{1,0:T(8,128)(2,1)S(1)}, u32[]{:S(2)}, u32[]{:S(2)}) collective-permute-start(bf16[768,768]{1,0:T(8,128)(2,1)} %collective-permute-done.1), channel_id=1, source_target_pairs={{0,1},{1,0},{2,3},{3,2},{4,5},{5,4},{6,7},{7,6},{8,9},{9,8},{10,11... | collective-permute-start | bytes 3538952 | tf_op jit(solution)/shard_map/ppermute | solution.py:150
  30.2 15.5 %copy-start.14 = (bf16[512,3072]{1,0:T(8,128)(2,1)S(1)}, bf16[512,3072]{1,0:T(8,128)(2,1)}, u32[]{:S(2)}) copy-start(bf16[512,3072]{1,0:T(8,128)(2,1)} %refs_3_.1) | copy-start | bytes 9437188
  32.6 61.5 %collective-permute-start.4 = (bf16[2,768,256]{2,1,0:T(8,128)(2,1)S(1)}, bf16[2,768,256]{2,1,0:T(8,128)(2,1)S(1)}, u32[]{:S(2)}, u32[]{:S(2)}) collective-permute-start(bf16[2,768,256]{2,1,0:T(8,128)(2,1)S(1)} %collective-permute-done.3.near), channel_id=1, source_target_pairs={{0,8},{8,16},{12,4},{16,24},{20,12},{28,20},{1,9},{9,17},{13,5},{1... | collective-permute-start | bytes 2359304 | tf_op jit(solution)/shard_map/ppermute | solution.py:156
  42.1 28.6 %collective-permute-start.6 = (bf16[2,768,256]{2,1,0:T(8,128)(2,1)S(1)}, bf16[2,768,256]{2,1,0:T(8,128)(2,1)S(1)}, u32[]{:S(2)}, u32[]{:S(2)}) collective-permute-start(bf16[2,768,256]{2,1,0:T(8,128)(2,1)S(1)} %collective-permute-done.5.near), channel_id=1, source_target_pairs={{0,8},{8,16},{12,4},{16,24},{20,12},{28,20},{1,9},{9,17},{13,5},{1... | collective-permute-start | bytes 2359304 | tf_op jit(solution)/shard_map/ppermute | solution.py:156
  49.8 20.8 %copy-start = (bf16[768,512]{1,0:T(8,128)(2,1)S(1)}, bf16[768,512]{1,0:T(8,128)(2,1)}, u32[]{:S(2)}) copy-start(bf16[768,512]{1,0:T(8,128)(2,1)} %km.3) | copy-start | bytes 2359300
  49.8 20.8 %copy-start.1 = (bf16[768,512]{1,0:T(8,128)(2,1)S(1)}, bf16[768,512]{1,0:T(8,128)(2,1)}, u32[]{:S(2)}) copy-start(bf16[768,512]{1,0:T(8,128)(2,1)} %vm.3) | copy-start | bytes 2359300
  49.9 20.8 %copy-start.2 = (bf16[768,512]{1,0:T(8,128)(2,1)S(1)}, bf16[768,512]{1,0:T(8,128)(2,1)}, u32[]{:S(2)}) copy-start(bf16[768,512]{1,0:T(8,128)(2,1)} %q.3) | copy-start | bytes 2359300
  70.7 18.6 %copy-start.11 = (bf16[768,768]{1,0:T(8,128)(2,1)S(1)}, bf16[768,768]{1,0:T(8,128)(2,1)}, u32[]{:S(2)}) copy-start(bf16[768,768]{1,0:T(8,128)(2,1)} %param.10) | copy-start | bytes 3538948
  89.2 4.9 %copy-start.3 = (f32[2,768,256]{2,1,0:T(8,128)}, f32[2,768,256]{2,1,0:T(8,128)S(1)}, u32[]{:S(2)}) copy-start(f32[2,768,256]{2,1,0:T(8,128)S(1)} %get-tuple-element.25.refs_9_) | copy-start | bytes 4718596
  89.3 4.9 %copy-start.4 = (f32[2,768,256]{2,1,0:T(8,128)}, f32[2,768,256]{2,1,0:T(8,128)S(1)}, u32[]{:S(2)}) copy-start(f32[2,768,256]{2,1,0:T(8,128)S(1)} %get-tuple-element.23.refs_7_) | copy-start | bytes 4718596
  89.3 4.9 %copy-start.7 = (bf16[2,768,256]{2,1,0:T(8,128)(2,1)}, bf16[2,768,256]{2,1,0:T(8,128)(2,1)S(1)}, u32[]{:S(2)}) copy-start(bf16[2,768,256]{2,1,0:T(8,128)(2,1)S(1)} %get-tuple-element.21.refs_5_) | copy-start | bytes 2359300
  89.3 4.9 %copy-start.9 = (bf16[768,256]{1,0:T(8,128)(2,1)}, bf16[768,256]{1,0:T(8,128)(2,1)S(1)}, u32[]{:S(2)}) copy-start(bf16[768,256]{1,0:T(8,128)(2,1)S(1)} %get-tuple-element.19.refs_1_) | copy-start | bytes 1179652
  112.6 1.2 copy-start.5
  113.8 1.3 copy-start.6
  115.0 0.9 copy-start.8
  115.9 0.7 copy-start.10
  210.0 1.6 copy-start.12
  210.9 1.6 copy-start.13

commit v3 on v2

--- a/solution.py
+++ b/solution.py
@@ -156,13 +156,38 @@
     return lax.ppermute(x, axis, [(i, j) for i, j in pairs if 0 <= j < size])
 
 
+def away_terms(turned, side, att, cols, out):
+    out[0] = dot_tn(att[...], cols[0]).astype(BF16)
+
+
+def away_call(turned, side, att, stacked, piece):
+    rows, part = att.shape
+    return pl.pallas_call(
+        away_terms,
+        grid_spec=pltpu.PrefetchScalarGridSpec(
+            num_scalar_prefetch=2,
+            grid=(4,),
+            in_specs=[
+                pl.BlockSpec((rows, part), lambda k, *_: (0, 0)),
+                pl.BlockSpec((1, rows, piece), lambda k, t, x: (t[k], 0, 1 - x[0])),
+            ],
+            out_specs=pl.BlockSpec((1, part, piece), lambda k, *_: (k, 0, 0)),
+        ),
+        out_shape=jax.ShapeDtypeStruct((4, part, piece), BF16),
+        compiler_params=pltpu.CompilerParams(dimension_semantics=("arbitrary",)),
+        cost_estimate=pl.CostEstimate(
+            flops=8 * rows * part * piece, bytes_accessed=rows * piece * 12, transcendentals=0
+        ),
+    )(turned, side, att, stacked)
+
+
 MESH = pl.DeviceIdType.MESH
 
 
 def finish(
     chunks, seq, norm,
-    att, stacked, weight, rim_far, rim_near, mid,
-    projected, dkv, grad_weight,
+    att, stacked, weight, rim_far, rim_near, mid, relay, crossed,
+    projected, dk, dv, grad_weight,
     far_in, near_out, near_in, gw_out, gw_in, gw_sum, two_out, two_in, four_out, four_in,
     core_out, core_in, mine, theirs, y_out, y_in,
     far_s, far_r, near_s, near_r, gw_s, gw_r, two_s, two_r, four_s, four_r, core_s, core_r, y_s, y_r,
@@ -204,12 +229,16 @@
     sends_far = (down >= 0) & (down < seq)
     up = s + 2 - 4 * x
     gets_far = (up >= 0) & (up < seq)
-    fars = [send(rim_far[c], far_in.at[c], far_s, far_r, c, (down, h)) for c in range(chunks)]
+    nears = [send(near_out.at[c], near_in.at[c], near_s, near_r, c, beside) for c in range(chunks)]
+    far = send(rim_far[1], far_in, far_s, far_r, 0, (down, h))
 
     @pl.when(sends_far)
     def _():
-        for copy in fars:
-            copy.start()
+        far.start()
+
+    for i in range(2):
+        near_out[0, i] = (rim_near[0][i] + relay[i].astype(F32)).astype(BF16)
+    nears[0].start()
 
     def columns(k, side):
         r = (h0 + z0 + k % 2) % 2 + 2 * ((h1 + z1 + k // 2) % 2)
@@ -218,8 +247,7 @@
     gws = []
     for k in (1, 3, 2, 0):
         cot = columns(k, 1 - x)
-        for c in range(chunks):
-            gw_out[k, c * part : (c + 1) * part] = dot_tn(att[c][...], cot).astype(BF16)
+        gw_out[k] = dot_tn(att[1][...], cot).astype(BF16)
         gws.append(send(gw_out.at[k], gw_in.at[k], gw_s, gw_r, k, beside))
         gws[-1].start()
 
@@ -242,27 +270,24 @@
     ys = send(y_out, y_in, y_s, y_r, 0, across)
     ys.start()
 
-    nears = []
-    for c in range(chunks):
-        nears.append(send(near_out.at[c], near_in.at[c], near_s, near_r, c, beside))
-
-        @pl.when(gets_far)
-        def _():
-            fars[c].wait_recv()
-            for i in range(2):
-                near_out[c, i] = (rim_near[c][i] + far_in[c, i].astype(F32)).astype(BF16)
-
-        @pl.when(jnp.logical_not(gets_far))
-        def _():
-            for i in range(2):
-                near_out[c, i] = rim_near[c][i].astype(BF16)
-
-        nears[c].start()
+    @pl.when(gets_far)
+    def _():
+        far.wait_recv()
+        for i in range(2):
+            near_out[1, i] = (rim_near[1][i] + far_in[i].astype(F32)).astype(BF16)
+
+    @pl.when(jnp.logical_not(gets_far))
+    def _():
+        for i in range(2):
+            near_out[1, i] = rim_near[1][i].astype(BF16)
+
+    nears[1].start()
 
     for k in range(4):
         cot = columns(k, x)
         for c in range(chunks):
             gw_sum[k, c * part : (c + 1) * part] = dot_tn(att[c][...], cot)
+        gw_sum[k, :part] += crossed[k].astype(F32)
     mine[...] = share(0)
     cores[1].wait_recv()
     mine[...] += core_in[1].astype(F32)
@@ -270,14 +295,15 @@
     twos = []
     for i, k in enumerate((1, 3)):
         gws[i].wait_recv()
-        two_out[i] = (gw_sum[k] + gw_in[k].astype(F32)).astype(BF16)
+        gw_sum[k, part:] += gw_in[k].astype(F32)
+        two_out[i] = gw_sum[k].astype(BF16)
         twos.append(send(two_out.at[i], two_in.at[i], two_s, two_r, i, hop2))
     twos[1].start()
     twos[0].start()
     gws[2].wait_recv()
-    gw_sum[2] += gw_in[2].astype(F32)
+    gw_sum[2, part:] += gw_in[2].astype(F32)
     gws[3].wait_recv()
-    gw_sum[0] += gw_in[0].astype(F32)
+    gw_sum[0, part:] += gw_in[0].astype(F32)
     twos[1].wait_recv()
     four_out[...] = (gw_sum[2] + two_in[1].astype(F32)).astype(BF16)
     four = send(four_out, four_in, four_s, four_r, 0, hop4)
@@ -291,19 +317,18 @@
     grad_weight[...] = (gw_sum[0] + four_in[...].astype(F32)) * norm
     for c in range(chunks):
         nears[c].wait_recv()
-        for i in range(2):
-            dkv[i, :, c * part : (c + 1) * part] = (mid[c][i] + near_in[c, i].astype(F32)).astype(BF16)
+        for i, out in enumerate((dk, dv)):
+            out[:, c * part : (c + 1) * part] = (mid[c][i] + near_in[c, i].astype(F32)).astype(BF16)
 
     @pl.when(sends_far)
     def _():
-        for copy in fars:
-            copy.wait_send()
+        far.wait_send()
 
     for copy in gws + cores + nears + twos + [ys, four]:
         copy.wait_send()
 
 
-def finish_call(atts, stacked, weight, fars, nears, mids, seq, norm):
+def finish_call(atts, stacked, weight, fars, nears, mids, relay, crossed, seq, norm):
     chunks = len(atts)
     rows, part = atts[0].shape
     depth = chunks * part
@@ -328,19 +353,20 @@
 
     return pl.pallas_call(
         kernel,
-        in_specs=[vmem] * (4 * chunks + 2),
-        out_specs=[vmem] * 3,
+        in_specs=[vmem] * (4 * chunks + 4),
+        out_specs=[vmem] * 4,
         out_shape=[
             jax.ShapeDtypeStruct((rows, width), BF16),
-            jax.ShapeDtypeStruct((2, rows, depth), BF16),
+            jax.ShapeDtypeStruct((rows, depth), BF16),
+            jax.ShapeDtypeStruct((rows, depth), BF16),
             jax.ShapeDtypeStruct((depth, piece), F32),
         ],
         scratch_shapes=[
+            pltpu.VMEM((2, RIM, part), BF16),
             pltpu.VMEM(rim, BF16),
             pltpu.VMEM(rim, BF16),
-            pltpu.VMEM(rim, BF16),
-            pltpu.VMEM((4, depth, piece), BF16),
-            pltpu.VMEM((4, depth, piece), BF16),
+            pltpu.VMEM((4, part, piece), BF16),
+            pltpu.VMEM((4, part, piece), BF16),
             pltpu.VMEM((4, depth, piece), F32),
             pltpu.VMEM((2, depth, piece), BF16),
             pltpu.VMEM((2, depth, piece), BF16),
@@ -352,7 +378,7 @@
             pltpu.VMEM((rows, width), F32),
             pltpu.VMEM((rows, width), BF16),
             pltpu.VMEM((rows, width), BF16),
-            sem((chunks,)), sem((chunks,)), sem((chunks,)), sem((chunks,)),
+            sem((1,)), sem((1,)), sem((chunks,)), sem((chunks,)),
             sem((4,)), sem((4,)), sem((2,)), sem((2,)), sem((1,)), sem((1,)),
             sem((2,)), sem((2,)), sem((1,)), sem((1,)),
         ],
@@ -362,7 +388,7 @@
         cost_estimate=pl.CostEstimate(
             flops=4 * rows * depth * width * 4, bytes_accessed=40 << 20, transcendentals=0
         ),
-    )(*atts, stacked, weight, *fars, *nears, *mids)
+    )(*atts, stacked, weight, *fars, *nears, *mids, relay, crossed)
 
 
 def local(queries, key_rows, value_rows, out_weight, cotangent, neighbours):
@@ -407,8 +433,19 @@
     count = jnp.sum(alive, axis=1).astype(jnp.int32)
 
     atts, dqs, mids, fars, nears = [], [], [], [], []
+    if paired:
+        stacked = jnp.stack(shards)
+        turned = ((h ^ (s // 2)) ^ jnp.arange(4, dtype=jnp.int32)).astype(jnp.int32)
+        side = (s % 2).astype(jnp.int32).reshape(1)
+        place, stacked = lax.optimization_barrier((place, stacked))
     for n in range(chunks):
         far, near = halos[n]
+        if n == 1 and paired:
+            place, relay = lax.optimization_barrier((place, fars[0]))
+            relay = shift(relay, "seq", -2)
+            away = away_call(turned, side, atts[0], stacked, piece)
+            place, away = lax.optimization_barrier((place, away))
+            crossed = swap(away, "seq", 1)
         att, dq, mid, rim_far, rim_near = attention_call(
             place, count, queries, grad_attention, key_rows, value_rows, far, near, n * per, per
         )
@@ -420,10 +457,10 @@
 
     grad_queries = jnp.concatenate(dqs, axis=1)
     if paired:
-        projected, dkv, grad_weight = finish_call(
-            atts, jnp.stack(shards), out_weight, fars, nears, mids, seq, norm
+        projected, grad_keys, grad_values, grad_weight = finish_call(
+            atts, stacked, out_weight, fars, nears, mids, relay, crossed, seq, norm
         )
-        return (projected, grad_queries, dkv[0], dkv[1], grad_weight)
+        return (projected, grad_queries, grad_keys, grad_values, grad_weight)
 
     dks, dvs = [], []
     for n in range(chunks):

time: 214 us -> 191 us (0.89)
  waiting for transfers between devices: 47.3 us -> 27.6 us
  Pallas kernels: 128 us -> 116 us
  local copies, waits for them, and re-layouts: 10.7 us -> 15.5 us
  starting transfers between devices: 12.4 us -> 15.2 us
    ppermute x2 -> x3, waiting for transfers between devices: 19.9 us -> 0.01 us  [shift(): return lax.ppermute(x, axis, [(i, j) for i, j in pairs if 0 <= j < size])]
    pallas_call x1 -> x2, Pallas kernels: 90.7 us -> 78.7 us  [the longest x1 73.6 us: finish_call(): pl.pallas_call(kernel, in_specs=[vmem] * (4 * chunks + 4), out_specs=[vme...]
    unnamed x34 -> x50, local copies, waits for them, and re-layouts: 6.59 us -> 13.9 us
    squeeze x1 -> x0, local copies, waits for them, and re-layouts: 2.61 us -> none  [local(): return (projected, grad_queries, dkv[0], dkv[1], grad_weight)]
    ppermute x2 -> x3, starting transfers between devices: 7.27 us -> 9.41 us  [shift(): return lax.ppermute(x, axis, [(i, j) for i, j in pairs if 0 <= j < size])]
    ppermute x5 -> x6, starting transfers between devices: 5.13 us -> 5.83 us  [swap(): lax.ppermute(x, axis, [(i, i ^ bit) for i in range(lax.axis_size(axis))])]
    ppermute x5 -> x6, waiting for transfers between devices: 27.4 us -> 27.6 us  [swap(): lax.ppermute(x, axis, [(i, i ^ bit) for i in range(lax.axis_size(axis))])]
  transfers between devices with their start and end apart: 7 -> 9, of which waited for: 3 -> 2; matrix products, arithmetic and copies ran while one was open for 7% -> 9% of each run, Pallas kernels for 9% -> 22%
where the time goes in v3:
time: 191 us
  Pallas kernels  116 us (61%)
  waiting for transfers between devices  27.6 us (14%)
  local copies, waits for them, and re-layouts  15.5 us (8%)
  starting transfers between devices  15.2 us (8%)
  matrix products  8.51 us (4%)
  other arithmetic  7.22 us (4%)
    pallas_call x1, Pallas kernels, finish_call(): pl.pallas_call(kernel, in_specs=[vmem] * (4 * chunks + 4), out_specs=[vme...  73.6 us
    pallas_call x2, Pallas kernels, attention_call(): pl.pallas_call(functools.partial(attend, rows, tiles), grid_spec=pltpu.Pr...  37.7 us
    ppermute x6, waiting for transfers between devices, swap(): lax.ppermute(x, axis, [(i, i ^ bit) for i in range(lax.axis_size(axis))])  27.6 us
    unnamed x50, local copies, waits for them, and re-layouts  13.9 us
    ppermute x3, starting transfers between devices, shift(): return lax.ppermute(x, axis, [(i, j) for i, j in pairs if 0 <= j < size])  9.41 us
    dot_general x4, matrix products, dot_nt(): lax.dot_general(a, b, (((1,), (1,)), ((), ())), preferred_element_type=F32)  8.51 us
    ppermute x6, starting transfers between devices, swap(): lax.ppermute(x, axis, [(i, i ^ bit) for i in range(lax.axis_size(axis))])  5.83 us
    pallas_call x1, Pallas kernels, away_call(): pl.pallas_call(away_terms, grid_spec=pltpu.PrefetchScalarGridSpec(num_sca...  5.11 us
  transfers between devices with their start and end apart: 9, of which 2 were waited for; matrix products, arithmetic and copies ran while one was open for 9% of the time, Pallas kernels for 22%

profile of v3, /device:TPU:0, one launch (start us, length us, event | category | flops | bytes accessed | tf_op | source)
XLA Modules:
  0.0 191.4 jit_solution(3655053030296586248)
XLA Ops:
  0.6 3.0 %collective-permute-start.1 = (bf16[768,768]{1,0:T(8,128)(2,1)}, bf16[768,768]{1,0:T(8,128)(2,1)}, u32[]{:S(2)}, u32[]{:S(2)}) collective-permute-start(bf16[768,768]{1,0:T(8,128)(2,1)} %param.10), channel_id=1, source_target_pairs={{0,2},{1,3},{2,0},{3,1},{4,6},{5,7},{6,4},{7,5},{8,10},{9,11},{10,... | collective-permute-start | bytes 3538952 | tf_op jit(solution)/shard_map/ppermute | solution.py:150
  3.7 0.0 collective-permute-start
  3.7 1.5 slice_bitcast_fusion
  5.1 0.0 copy-start.22
  5.1 0.0 copy-start.16
  5.1 0.9 pad_maximum_fusion.1
  6.1 1.5 collective-permute-start.3
  7.6 0.9 pad_maximum_fusion.2
  8.5 0.5 collective-permute-start.5
  9.1 20.9 %collective-permute-done.1 = bf16[768,768]{1,0:T(8,128)(2,1)} collective-permute-done((bf16[768,768]{1,0:T(8,128)(2,1)}, bf16[768,768]{1,0:T(8,128)(2,1)}, u32[]{:S(2)}, u32[]{:S(2)}) %collective-permute-start.1) | collective-permute-done | bytes 1179680 | tf_op jit(solution)/shard_map/ppermute | solution.py:150
  29.9 0.0 collective-permute-start.2
  30.0 0.1 convert_reduce_fusion
  30.1 0.1 reshape.16.place
  30.2 0.5 iota_xor_fusion.turned
  30.7 2.1 %fusion.6 = f32[512,768]{0,1:T(8,128)S(1)} fusion(bf16[768,768]{1,0:T(8,128)(2,1)S(1)} %copy-done.16, bf16[512,3072]{1,0:T(8,128)(2,1)} %refs_3_.1, s32[]{:T(128)S(6)} %select_n.50), kind=kOutput, calls=%fused_computation.11 | convolution fusion | flops 603979776 | bytes 3538948 | tf_op jit(solution)/shard_map/dot_general | solution.py:21
  32.8 0.0 copy-start.12
  32.8 3.7 %collective-permute-start.4 = (bf16[2,768,256]{2,1,0:T(8,128)(2,1)S(1)}, bf16[2,768,256]{2,1,0:T(8,128)(2,1)S(1)}, u32[]{:S(2)}, u32[]{:S(2)}) collective-permute-start(bf16[2,768,256]{2,1,0:T(8,128)(2,1)S(1)} %collective-permute-done.3.near), channel_id=1, source_target_pairs={{0,8},{8,16},{12,4},{16,24},{20,12},{28,20},{1,9},{9,17},{13,5},{1... | collective-permute-start | bytes 2359304 | tf_op jit(solution)/shard_map/ppermute | solution.py:156
  36.5 6.7 %collective-permute-done.5.near = bf16[2,768,256]{2,1,0:T(8,128)(2,1)} collective-permute-done((bf16[2,768,256]{2,1,0:T(8,128)(2,1)}, bf16[2,768,256]{2,1,0:T(8,128)(2,1)}, u32[]{:S(2)}, u32[]{:S(2)}) %collective-permute-start.5) | collective-permute-done | bytes 786464 | tf_op jit(solution)/shard_map/ppermute | solution.py:150
  43.2 4.4 %collective-permute-start.6 = (bf16[2,768,256]{2,1,0:T(8,128)(2,1)}, bf16[2,768,256]{2,1,0:T(8,128)(2,1)}, u32[]{:S(2)}, u32[]{:S(2)}) collective-permute-start(bf16[2,768,256]{2,1,0:T(8,128)(2,1)} %collective-permute-done.5.near), channel_id=1, source_target_pairs={{0,8},{8,16},{12,4},{16,24},{20,12},{28,20},{1,9},{9,17},{13,5},{1... | collective-permute-start | bytes 2359304 | tf_op jit(solution)/shard_map/ppermute | solution.py:156
  47.6 2.1 %fusion.2 = f32[512,768]{0,1:T(8,128)S(1)} fusion(bf16[768,768]{1,0:T(8,128)(2,1)} %collective-permute-done.1, bf16[512,3072]{1,0:T(8,128)(2,1)S(1)} %copy-done.14, s32[]{:T(128)S(6)} %select_n.52), kind=kOutput, calls=%fused_computation.7 | convolution fusion | flops 603979776 | bytes 3538948 | tf_op jit(solution)/shard_map/dot_general | solution.py:21
  49.7 2.1 %fusion.4 = f32[512,768]{0,1:T(8,128)S(1)} fusion(bf16[768,768]{1,0:T(8,128)(2,1)} %collective-permute-done, bf16[512,3072]{1,0:T(8,128)(2,1)S(1)} %copy-done.14, s32[]{:T(128)S(6)} %select_n.51), kind=kOutput, calls=%fused_computation.9 | convolution fusion | flops 603979776 | bytes 3538948 | tf_op jit(solution)/shard_map/dot_general | solution.py:21
  51.8 0.0 copy-start.15
  51.8 1.0 copy-done.15
  52.8 3.7 %pad_maximum_fusion.cols.refs_2_ = bf16[4,768,768]{2,1,0:T(8,128)(2,1)} fusion(bf16[1,768,768]{2,1,0:T(8,128)(2,1)S(1)} %bitcast.19, bf16[1,768,768]{2,1,0:T(8,128)(2,1)} %bitcast.2, bf16[1,768,768]{2,1,0:T(8,128)(2,1)} %bitcast.1, bf16[1,768,768]{2,1,0:T(8,128)(2,1)S(1)} %bitcast.20), kind=kLoop, calls=%fused_computation | loop fusion | flops 7077888 | bytes 9437184 | tf_op jit(solution)/shard_map/stack | solution.py:437
  56.5 0.0 copy-start.13
  56.5 2.3 %fusion.g = bf16[768,512]{1,0:T(8,128)(2,1)S(1)} fusion(bf16[768,768]{1,0:T(8,128)(2,1)} %copy-done.15, f32[512,768]{0,1:T(8,128)S(1)} %fusion.2, f32[512,768]{0,1:T(8,128)S(1)} %fusion.6, f32[512,768]{0,1:T(8,128)S(1)} %fusion.4, bf16[512,3072]{1,0:T(8,128)(2,1)S(1)} %copy-done.14, s32[]{:T(128)S(6)} %select_n.53), kind=kOutput, calls=%fused_computation.2 | convolution fusion | flops 605552640 | bytes 7471108 | tf_op jit(solution)/shard_map/dot_general | solution.py:21
  58.8 18.4 %shard_map.101 = (bf16[768,256]{1,0:T(8,128)(2,1)S(1)}, bf16[768,256]{1,0:T(8,128)(2,1)S(1)}, f32[2,768,256]{2,1,0:T(8,128)S(1)}, bf16[2,768,256]{2,1,0:T(8,128)(2,1)S(1)}, f32[2,768,256]{2,1,0:T(8,128)S(1)}) custom-call(s32[8]{0:T(128)S(1)} %reshape.16.place, s32[2]{0:T(128)S(1)} %get-tuple-element.49.count, bf16[768,512]{1,0:T(8,128)(2,1)S(1)} %copy-done.10, ...), custom_call_target="tpu_custom_call" | custom-call | flops 3623878656 | bytes 7864320 | tf_op jit(solution)/shard_map/pallas_call | solution.py:116
  77.3 1.1 copy-done
  78.4 1.2 copy-done.1
  79.6 0.8 copy-done.4
  80.4 5.1 %shard_map.102 = bf16[4,256,384]{2,1,0:T(8,128)(2,1)} custom-call(s32[4]{0:T(128)} %iota_xor_fusion.turned, s32[1]{0:T(128)} %bitcast.7.side, bf16[768,256]{1,0:T(8,128)(2,1)} %copy-done.4, bf16[4,768,768]{2,1,0:T(8,128)(2,1)} %pad_maximum_fusion.cols.refs_2_), custom_call_target="tpu_custom_call" | custom-call | flops 603979776 | bytes 3538944 | tf_op jit(solution)/shard_map/pallas_call | solution.py:165
  85.5 0.8 collective-permute-start.8
  86.3 1.3 collective-permute-start.7
  87.6 0.0 copy-start.11
  87.6 1.1 copy-done.11
  88.7 19.3 %shard_map.103 = (bf16[768,256]{1,0:T(8,128)(2,1)S(1)}, bf16[768,256]{1,0:T(8,128)(2,1)S(1)}, f32[2,768,256]{2,1,0:T(8,128)S(1)}, bf16[2,768,256]{2,1,0:T(8,128)(2,1)S(1)}, f32[2,768,256]{2,1,0:T(8,128)S(1)}) custom-call(s32[8]{0:T(128)S(1)} %reshape.16.place, s32[2]{0:T(128)S(1)} %get-tuple-element.49.count, bf16[768,512]{1,0:T(8,128)(2,1)S(1)} %copy-done.11, ...), custom_call_target="tpu_custom_call" | custom-call | flops 3623878656 | bytes 7864320 | tf_op jit(solution)/shard_map/pallas_call | solution.py:116
  108.0 1.1 copy-done.2
  109.2 1.2 copy-done.3
  110.4 1.0 pad_maximum_fusion.3
  111.5 0.1 copy-done.6
  111.6 0.1 copy-done.9
  111.7 0.6 copy-done.17
  112.3 0.3 copy-done.18
  112.6 73.6 %shard_map.104 = (bf16[768,768]{1,0:T(8,128)(2,1)}, bf16[768,512]{1,0:T(8,128)(2,1)}, bf16[768,512]{1,0:T(8,128)(2,1)}, f32[512,384]{1,0:T(8,128)}) custom-call(bf16[768,256]{1,0:T(8,128)(2,1)} %copy-done.4, bf16[768,256]{1,0:T(8,128)(2,1)} %copy-done.9, bf16[4,768,768]{2,1,0:T(8,128)(2,1)} %pad_maximum_fusion.cols.refs_2_, bf16[512,3072]{1,0:T(8,128)(2,1)} %refs_3_.1, ...), custom_call_target="tpu_custom_call" | custom-call | flops 4831838208 | bytes 41943040 | tf_op jit(solution)/shard_map/pallas_call | solution.py:354
  186.3 2.5 %copy.23 = bf16[768,768]{1,0:T(8,128)(2,1)} copy(bf16[768,768]{1,0:T(8,128)(2,1)} %get-tuple-element.58) | data formatting | bytes 2359296
  188.7 0.9 copy.24
  189.6 0.9 copy.25
  190.5 0.9 copy.26
  (36 shorter events, 0.1 us)
Async XLA Ops:
  0.6 29.3 %collective-permute-start.1 = (bf16[768,768]{1,0:T(8,128)(2,1)}, bf16[768,768]{1,0:T(8,128)(2,1)}, u32[]{:S(2)}, u32[]{:S(2)}) collective-permute-start(bf16[768,768]{1,0:T(8,128)(2,1)} %param.10), channel_id=1, source_target_pairs={{0,2},{1,3},{2,0},{3,1},{4,6},{5,7},{6,4},{7,5},{8,10},{9,11},{10,... | collective-permute-start | bytes 3538952 | tf_op jit(solution)/shard_map/ppermute | solution.py:150
  3.7 46.0 %collective-permute-start = (bf16[768,768]{1,0:T(8,128)(2,1)}, bf16[768,768]{1,0:T(8,128)(2,1)}, u32[]{:S(2)}, u32[]{:S(2)}) collective-permute-start(bf16[768,768]{1,0:T(8,128)(2,1)} %param.10), channel_id=1, source_target_pairs={{0,1},{1,0},{2,3},{3,2},{4,5},{5,4},{6,7},{7,6},{8,9},{9,8},{10,11... | collective-permute-start | bytes 3538952 | tf_op jit(solution)/shard_map/ppermute | solution.py:150
  5.1 24.8 %copy-start.22 = (s32[2,4]{1,0:T(2,128)S(1)}, s32[2,4]{1,0:T(2,128)}, u32[]{:S(2)}) copy-start(s32[2,4]{1,0:T(2,128)} %param.11) | copy-start | bytes 100
  5.1 25.5 %copy-start.16 = (bf16[768,768]{1,0:T(8,128)(2,1)S(1)}, bf16[768,768]{1,0:T(8,128)(2,1)}, u32[]{:S(2)}) copy-start(bf16[768,768]{1,0:T(8,128)(2,1)} %param.10) | copy-start | bytes 3538948
  6.1 26.7 %collective-permute-start.3 = (bf16[2,768,256]{2,1,0:T(8,128)(2,1)}, bf16[2,768,256]{2,1,0:T(8,128)(2,1)S(1)}, u32[]{:S(2)}, u32[]{:S(2)}) collective-permute-start(bf16[2,768,256]{2,1,0:T(8,128)(2,1)} %pad_maximum_fusion.1), channel_id=1, source_target_pairs={{0,4},{4,0},{8,12},{12,8},{16,20},{20,16},{24,28},{28,24},{1,5},{5... | collective-permute-start | bytes 2359304 | tf_op jit(solution)/shard_map/ppermute | solution.py:150
  8.5 34.7 %collective-permute-start.5 = (bf16[2,768,256]{2,1,0:T(8,128)(2,1)}, bf16[2,768,256]{2,1,0:T(8,128)(2,1)}, u32[]{:S(2)}, u32[]{:S(2)}) collective-permute-start(bf16[2,768,256]{2,1,0:T(8,128)(2,1)} %pad_maximum_fusion.2), channel_id=1, source_target_pairs={{0,4},{4,0},{8,12},{12,8},{16,20},{20,16},{24,28},{28,24},{1,5},{5... | collective-permute-start | bytes 2359304 | tf_op jit(solution)/shard_map/ppermute | solution.py:150
  29.9 21.9 %collective-permute-start.2 = (bf16[768,768]{1,0:T(8,128)(2,1)}, bf16[768,768]{1,0:T(8,128)(2,1)S(1)}, u32[]{:S(2)}, u32[]{:S(2)}) collective-permute-start(bf16[768,768]{1,0:T(8,128)(2,1)} %collective-permute-done.1), channel_id=1, source_target_pairs={{0,1},{1,0},{2,3},{3,2},{4,5},{5,4},{6,7},{7,6},{8,9},{9,8},{10,11... | collective-permute-start | bytes 3538952 | tf_op jit(solution)/shard_map/ppermute | solution.py:150
  30.7 16.9 %copy-start.14 = (bf16[512,3072]{1,0:T(8,128)(2,1)S(1)}, bf16[512,3072]{1,0:T(8,128)(2,1)}, u32[]{:S(2)}) copy-start(bf16[512,3072]{1,0:T(8,128)(2,1)} %refs_3_.1) | copy-start | bytes 9437188
  32.8 16.9 %copy-start.12 = (bf16[2,768,256]{2,1,0:T(8,128)(2,1)}, bf16[2,768,256]{2,1,0:T(8,128)(2,1)S(1)}, u32[]{:S(2)}) copy-start(bf16[2,768,256]{2,1,0:T(8,128)(2,1)S(1)} %collective-permute-done.3.near) | copy-start | bytes 2359300
  32.8 26.0 %collective-permute-start.4 = (bf16[2,768,256]{2,1,0:T(8,128)(2,1)S(1)}, bf16[2,768,256]{2,1,0:T(8,128)(2,1)S(1)}, u32[]{:S(2)}, u32[]{:S(2)}) collective-permute-start(bf16[2,768,256]{2,1,0:T(8,128)(2,1)S(1)} %collective-permute-done.3.near), channel_id=1, source_target_pairs={{0,8},{8,16},{12,4},{16,24},{20,12},{28,20},{1,9},{9,17},{13,5},{1... | collective-permute-start | bytes 2359304 | tf_op jit(solution)/shard_map/ppermute | solution.py:156
  43.2 44.3 %collective-permute-start.6 = (bf16[2,768,256]{2,1,0:T(8,128)(2,1)}, bf16[2,768,256]{2,1,0:T(8,128)(2,1)}, u32[]{:S(2)}, u32[]{:S(2)}) collective-permute-start(bf16[2,768,256]{2,1,0:T(8,128)(2,1)} %collective-permute-done.5.near), channel_id=1, source_target_pairs={{0,8},{8,16},{12,4},{16,24},{20,12},{28,20},{1,9},{9,17},{13,5},{1... | collective-permute-start | bytes 2359304 | tf_op jit(solution)/shard_map/ppermute | solution.py:156
  51.8 1.0 copy-start.15
  56.5 2.3 %copy-start.7 = (bf16[768,512]{1,0:T(8,128)(2,1)S(1)}, bf16[768,512]{1,0:T(8,128)(2,1)}, u32[]{:S(2)}) copy-start(bf16[768,512]{1,0:T(8,128)(2,1)} %km.3) | copy-start | bytes 2359300
  56.5 2.3 %copy-start.8 = (bf16[768,512]{1,0:T(8,128)(2,1)S(1)}, bf16[768,512]{1,0:T(8,128)(2,1)}, u32[]{:S(2)}) copy-start(bf16[768,512]{1,0:T(8,128)(2,1)} %vm.3) | copy-start | bytes 2359300
  56.5 2.3 %copy-start.10 = (bf16[768,512]{1,0:T(8,128)(2,1)S(1)}, bf16[768,512]{1,0:T(8,128)(2,1)}, u32[]{:S(2)}) copy-start(bf16[768,512]{1,0:T(8,128)(2,1)} %q.3) | copy-start | bytes 2359300
  56.5 2.3 %copy-start.13 = (bf16[2,768,256]{2,1,0:T(8,128)(2,1)S(1)}, bf16[2,768,256]{2,1,0:T(8,128)(2,1)}, u32[]{:S(2)}) copy-start(bf16[2,768,256]{2,1,0:T(8,128)(2,1)} %copy-done.12) | copy-start | bytes 2359300
  77.3 1.1 copy-start
  78.4 1.2 copy-start.1
  79.6 0.8 copy-start.4
  80.4 5.9 %copy-start.5 = (bf16[2,768,256]{2,1,0:T(8,128)(2,1)}, bf16[2,768,256]{2,1,0:T(8,128)(2,1)S(1)}, u32[]{:S(2)}) copy-start(bf16[2,768,256]{2,1,0:T(8,128)(2,1)S(1)} %get-tuple-element.37.refs_4_) | copy-start | bytes 2359300
  85.5 25.9 %collective-permute-start.8 = (bf16[4,256,384]{2,1,0:T(8,128)(2,1)}, bf16[4,256,384]{2,1,0:T(8,128)(2,1)S(1)}, u32[]{:S(2)}, u32[]{:S(2)}) collective-permute-start(bf16[4,256,384]{2,1,0:T(8,128)(2,1)} %shard_map.102), channel_id=1, source_target_pairs={{0,4},{4,0},{8,12},{12,8},{16,20},{20,16},{24,28},{28,24},{1,5},{5... | collective-permute-start | bytes 2359304 | tf_op jit(solution)/shard_map/ppermute | solution.py:150
  86.3 25.2 %collective-permute-start.7 = (bf16[2,768,256]{2,1,0:T(8,128)(2,1)S(1)}, bf16[2,768,256]{2,1,0:T(8,128)(2,1)S(1)}, u32[]{:S(2)}, u32[]{:S(2)}) collective-permute-start(bf16[2,768,256]{2,1,0:T(8,128)(2,1)S(1)} %get-tuple-element.37.refs_4_), channel_id=1, source_target_pairs={{4,12},{8,0},{12,20},{16,8},{20,28},{24,16},{5,13},{9,1},{13,21},{... | collective-permute-start | bytes 2359304 | tf_op jit(solution)/shard_map/ppermute | solution.py:156
  87.6 1.1 copy-start.11
  108.0 1.2 copy-start.2
  109.2 1.2 copy-start.3
  110.4 1.1 copy-start.6
  110.4 1.3 copy-start.9
  111.4 0.9 copy-start.17
  111.6 1.0 copy-start.18
  186.2 2.5 %copy-start.21 = (bf16[768,512]{1,0:T(8,128)(2,1)S(1)}, bf16[768,512]{1,0:T(8,128)(2,1)}, u32[]{:S(2)}) copy-start(bf16[768,512]{1,0:T(8,128)(2,1)} %get-tuple-element.60) | copy-start | bytes 2359300
  186.2 3.4 %copy-start.20 = (bf16[768,512]{1,0:T(8,128)(2,1)S(1)}, bf16[768,512]{1,0:T(8,128)(2,1)}, u32[]{:S(2)}) copy-start(bf16[768,512]{1,0:T(8,128)(2,1)} %get-tuple-element.61) | copy-start | bytes 2359300
  188.7 1.8 copy-start.19

commit v4 on v3

--- a/solution.py
+++ b/solution.py
@@ -60,12 +60,19 @@
     def at(j):
         return pl.ds(pl.multiple_of(place[t * SLOTS + j] * TILE, TILE), TILE)
 
+    def slots(step, carry):
+        for j in range(SLOTS):
+            carry = step(j, carry)
+        return carry
+
     def score(j, m):
         s = dot_nt(qv, kx[at(j), :])
+        if j:
+            s = jnp.where(j < live, s, -1e30)
         scr[j] = s
         return jnp.maximum(m, fold(jnp.maximum, s))
 
-    m = lax.fori_loop(0, live, score, jnp.full((TILE, HD), -3e38, F32))
+    m = slots(score, jnp.full((TILE, HD), -3e38, F32))
     m = jnp.max(m, axis=1, keepdims=True)
 
     def soft(j, carry):
@@ -75,7 +82,7 @@
         return total + fold(jnp.add, e), acc + dot_nn(e.astype(BF16), vx[at(j), :])
 
     zero = jnp.zeros((TILE, HD), F32)
-    total, acc = lax.fori_loop(0, live, soft, (zero, zero))
+    total, acc = slots(soft, (zero, zero))
     inv = 1.0 / jnp.sum(total, axis=1, keepdims=True)
     out = (acc * inv).astype(BF16)
     att[...] = out
@@ -90,7 +97,7 @@
         dk[here, :] += dot_tn(ds, qv)
         return acc + dot_nn(ds, k)
 
-    dq[...] = (lax.fori_loop(0, live, back, zero) * scale).astype(BF16)
+    dq[...] = (slots(back, zero) * scale).astype(BF16)
 
     @pl.when(t == tiles - 1)
     def _():

time: 191 us -> 175 us (0.916)
  Pallas kernels: 116 us -> 100 us
    pallas_call x2, Pallas kernels: 37.7 us -> 29.3 us  [attention_call(): pl.pallas_call(functools.partial(attend, rows, tiles), grid_spec=pltpu.Pr...]
    pallas_call x1, Pallas kernels: 73.6 us -> 66.1 us  [finish_call(): pl.pallas_call(kernel, in_specs=[vmem] * (4 * chunks + 4), out_specs=[vme...]
  transfers between devices with their start and end apart: 9 -> 9, of which waited for: 2 -> 2; matrix products, arithmetic and copies ran while one was open for 9% -> 10% of each run, Pallas kernels for 22% -> 20%
where the time goes in v4:
time: 175 us
  Pallas kernels  100 us (57%)
  waiting for transfers between devices  27.6 us (16%)
  local copies, waits for them, and re-layouts  15.5 us (9%)
  starting transfers between devices  14.7 us (8%)
  matrix products  8.51 us (5%)
  other arithmetic  7.22 us (4%)
    pallas_call x1, Pallas kernels, finish_call(): pl.pallas_call(kernel, in_specs=[vmem] * (4 * chunks + 4), out_specs=[vme...  66.1 us
    pallas_call x2, Pallas kernels, attention_call(): pl.pallas_call(functools.partial(attend, rows, tiles), grid_spec=pltpu.Pr...  29.3 us
    ppermute x6, waiting for transfers between devices, swap(): lax.ppermute(x, axis, [(i, i ^ bit) for i in range(lax.axis_size(axis))])  27.6 us
    unnamed x50, local copies, waits for them, and re-layouts  13.9 us
    ppermute x3, starting transfers between devices, shift(): return lax.ppermute(x, axis, [(i, j) for i, j in pairs if 0 <= j < size])  9.59 us
    dot_general x4, matrix products, dot_nt(): lax.dot_general(a, b, (((1,), (1,)), ((), ())), preferred_element_type=F32)  8.51 us
    pallas_call x1, Pallas kernels, away_call(): pl.pallas_call(away_terms, grid_spec=pltpu.PrefetchScalarGridSpec(num_sca...  5.11 us
    ppermute x6, starting transfers between devices, swap(): lax.ppermute(x, axis, [(i, i ^ bit) for i in range(lax.axis_size(axis))])  5.07 us
  transfers between devices with their start and end apart: 9, of which 2 were waited for; matrix products, arithmetic and copies ran while one was open for 10% of the time, Pallas kernels for 20%

profile of v4, /device:TPU:0, one launch (start us, length us, event | category | flops | bytes accessed | tf_op | source)
XLA Modules:
  0.0 174.8 jit_solution(7222306768416303654)
XLA Ops:
  0.6 3.0 %collective-permute-start.1 = (bf16[768,768]{1,0:T(8,128)(2,1)}, bf16[768,768]{1,0:T(8,128)(2,1)}, u32[]{:S(2)}, u32[]{:S(2)}) collective-permute-start(bf16[768,768]{1,0:T(8,128)(2,1)} %param.10), channel_id=1, source_target_pairs={{0,2},{1,3},{2,0},{3,1},{4,6},{5,7},{6,4},{7,5},{8,10},{9,11},{10,... | collective-permute-start | bytes 3538952 | tf_op jit(solution)/shard_map/ppermute | solution.py:157
  3.7 0.0 collective-permute-start
  3.7 1.5 slice_bitcast_fusion
  5.1 0.0 copy-start.22
  5.1 0.0 copy-start.16
  5.1 0.9 pad_maximum_fusion.1
  6.1 1.5 collective-permute-start.3
  7.6 0.9 pad_maximum_fusion.2
  8.5 0.5 collective-permute-start.5
  9.1 20.9 %collective-permute-done.1 = bf16[768,768]{1,0:T(8,128)(2,1)} collective-permute-done((bf16[768,768]{1,0:T(8,128)(2,1)}, bf16[768,768]{1,0:T(8,128)(2,1)}, u32[]{:S(2)}, u32[]{:S(2)}) %collective-permute-start.1) | collective-permute-done | bytes 1179680 | tf_op jit(solution)/shard_map/ppermute | solution.py:157
  29.9 0.0 collective-permute-start.2
  30.0 0.1 convert_reduce_fusion
  30.1 0.1 reshape.16.place
  30.2 0.5 iota_xor_fusion.turned
  30.7 2.1 %fusion.6 = f32[512,768]{0,1:T(8,128)S(1)} fusion(bf16[768,768]{1,0:T(8,128)(2,1)S(1)} %copy-done.16, bf16[512,3072]{1,0:T(8,128)(2,1)} %refs_3_.1, s32[]{:T(128)S(6)} %select_n.50), kind=kOutput, calls=%fused_computation.11 | convolution fusion | flops 603979776 | bytes 3538948 | tf_op jit(solution)/shard_map/dot_general | solution.py:21
  32.8 0.0 copy-start.12
  32.8 3.7 %collective-permute-start.4 = (bf16[2,768,256]{2,1,0:T(8,128)(2,1)S(1)}, bf16[2,768,256]{2,1,0:T(8,128)(2,1)S(1)}, u32[]{:S(2)}, u32[]{:S(2)}) collective-permute-start(bf16[2,768,256]{2,1,0:T(8,128)(2,1)S(1)} %collective-permute-done.3.near), channel_id=1, source_target_pairs={{0,8},{8,16},{12,4},{16,24},{20,12},{28,20},{1,9},{9,17},{13,5},{1... | collective-permute-start | bytes 2359304 | tf_op jit(solution)/shard_map/ppermute | solution.py:163
  36.5 6.7 %collective-permute-done.5.near = bf16[2,768,256]{2,1,0:T(8,128)(2,1)} collective-permute-done((bf16[2,768,256]{2,1,0:T(8,128)(2,1)}, bf16[2,768,256]{2,1,0:T(8,128)(2,1)}, u32[]{:S(2)}, u32[]{:S(2)}) %collective-permute-start.5) | collective-permute-done | bytes 786464 | tf_op jit(solution)/shard_map/ppermute | solution.py:157
  43.2 4.4 %collective-permute-start.6 = (bf16[2,768,256]{2,1,0:T(8,128)(2,1)}, bf16[2,768,256]{2,1,0:T(8,128)(2,1)}, u32[]{:S(2)}, u32[]{:S(2)}) collective-permute-start(bf16[2,768,256]{2,1,0:T(8,128)(2,1)} %collective-permute-done.5.near), channel_id=1, source_target_pairs={{0,8},{8,16},{12,4},{16,24},{20,12},{28,20},{1,9},{9,17},{13,5},{1... | collective-permute-start | bytes 2359304 | tf_op jit(solution)/shard_map/ppermute | solution.py:163
  47.6 2.1 %fusion.2 = f32[512,768]{0,1:T(8,128)S(1)} fusion(bf16[768,768]{1,0:T(8,128)(2,1)} %collective-permute-done.1, bf16[512,3072]{1,0:T(8,128)(2,1)S(1)} %copy-done.14, s32[]{:T(128)S(6)} %select_n.52), kind=kOutput, calls=%fused_computation.7 | convolution fusion | flops 603979776 | bytes 3538948 | tf_op jit(solution)/shard_map/dot_general | solution.py:21
  49.7 0.0 collective-permute-done
  49.7 2.1 %fusion.4 = f32[512,768]{0,1:T(8,128)S(1)} fusion(bf16[768,768]{1,0:T(8,128)(2,1)} %collective-permute-done, bf16[512,3072]{1,0:T(8,128)(2,1)S(1)} %copy-done.14, s32[]{:T(128)S(6)} %select_n.51), kind=kOutput, calls=%fused_computation.9 | convolution fusion | flops 603979776 | bytes 3538948 | tf_op jit(solution)/shard_map/dot_general | solution.py:21
  51.8 0.0 copy-start.15
  51.8 1.0 copy-done.15
  52.8 3.7 %pad_maximum_fusion.cols.refs_2_ = bf16[4,768,768]{2,1,0:T(8,128)(2,1)} fusion(bf16[1,768,768]{2,1,0:T(8,128)(2,1)S(1)} %bitcast.19, bf16[1,768,768]{2,1,0:T(8,128)(2,1)} %bitcast.2, bf16[1,768,768]{2,1,0:T(8,128)(2,1)} %bitcast.1, bf16[1,768,768]{2,1,0:T(8,128)(2,1)S(1)} %bitcast.20), kind=kLoop, calls=%fused_computation | loop fusion | flops 7077888 | bytes 9437184 | tf_op jit(solution)/shard_map/stack | solution.py:444
  56.5 0.0 copy-start.13
  56.5 2.3 %fusion.g = bf16[768,512]{1,0:T(8,128)(2,1)S(1)} fusion(bf16[768,768]{1,0:T(8,128)(2,1)} %copy-done.15, f32[512,768]{0,1:T(8,128)S(1)} %fusion.2, f32[512,768]{0,1:T(8,128)S(1)} %fusion.6, f32[512,768]{0,1:T(8,128)S(1)} %fusion.4, bf16[512,3072]{1,0:T(8,128)(2,1)S(1)} %copy-done.14, s32[]{:T(128)S(6)} %select_n.53), kind=kOutput, calls=%fused_computation.2 | convolution fusion | flops 605552640 | bytes 7471108 | tf_op jit(solution)/shard_map/dot_general | solution.py:21
  58.8 14.2 %shard_map.101 = (bf16[768,256]{1,0:T(8,128)(2,1)S(1)}, bf16[768,256]{1,0:T(8,128)(2,1)S(1)}, f32[2,768,256]{2,1,0:T(8,128)S(1)}, bf16[2,768,256]{2,1,0:T(8,128)(2,1)S(1)}, f32[2,768,256]{2,1,0:T(8,128)S(1)}) custom-call(s32[8]{0:T(128)S(1)} %reshape.16.place, s32[2]{0:T(128)S(1)} %get-tuple-element.49.count, bf16[768,512]{1,0:T(8,128)(2,1)S(1)} %copy-done.10, ...), custom_call_target="tpu_custom_call" | custom-call | flops 3623878656 | bytes 7864320 | tf_op jit(solution)/shard_map/pallas_call | solution.py:123
  73.1 1.1 copy-done
  74.2 1.2 copy-done.1
  75.4 0.8 copy-done.4
  76.2 5.1 %shard_map.102 = bf16[4,256,384]{2,1,0:T(8,128)(2,1)} custom-call(s32[4]{0:T(128)} %iota_xor_fusion.turned, s32[1]{0:T(128)} %bitcast.7.side, bf16[768,256]{1,0:T(8,128)(2,1)} %copy-done.4, bf16[4,768,768]{2,1,0:T(8,128)(2,1)} %pad_maximum_fusion.cols.refs_2_), custom_call_target="tpu_custom_call" | custom-call | flops 603979776 | bytes 3538944 | tf_op jit(solution)/shard_map/pallas_call | solution.py:172
  81.3 1.5 collective-permute-start.7
  82.8 0.0 copy-start.11
  82.8 1.1 copy-done.11
  83.9 15.0 %shard_map.103 = (bf16[768,256]{1,0:T(8,128)(2,1)S(1)}, bf16[768,256]{1,0:T(8,128)(2,1)S(1)}, f32[2,768,256]{2,1,0:T(8,128)S(1)}, bf16[2,768,256]{2,1,0:T(8,128)(2,1)S(1)}, f32[2,768,256]{2,1,0:T(8,128)S(1)}) custom-call(s32[8]{0:T(128)S(1)} %reshape.16.place, s32[2]{0:T(128)S(1)} %get-tuple-element.49.count, bf16[768,512]{1,0:T(8,128)(2,1)S(1)} %copy-done.11, ...), custom_call_target="tpu_custom_call" | custom-call | flops 3623878656 | bytes 7864320 | tf_op jit(solution)/shard_map/pallas_call | solution.py:123
  99.0 1.1 copy-done.2
  100.1 1.2 copy-done.3
  101.4 1.0 pad_maximum_fusion.3
  102.4 0.1 copy-done.6
  102.5 0.1 copy-done.9
  102.6 0.6 copy-done.17
  103.3 0.3 copy-done.18
  103.5 66.1 %shard_map.104 = (bf16[768,768]{1,0:T(8,128)(2,1)}, bf16[768,512]{1,0:T(8,128)(2,1)}, bf16[768,512]{1,0:T(8,128)(2,1)}, f32[512,384]{1,0:T(8,128)}) custom-call(bf16[768,256]{1,0:T(8,128)(2,1)} %copy-done.4, bf16[768,256]{1,0:T(8,128)(2,1)} %copy-done.9, bf16[4,768,768]{2,1,0:T(8,128)(2,1)} %pad_maximum_fusion.cols.refs_2_, bf16[512,3072]{1,0:T(8,128)(2,1)} %refs_3_.1, ...), custom_call_target="tpu_custom_call" | custom-call | flops 4831838208 | bytes 41943040 | tf_op jit(solution)/shard_map/pallas_call | solution.py:361
  169.6 2.5 %copy.23 = bf16[768,768]{1,0:T(8,128)(2,1)} copy(bf16[768,768]{1,0:T(8,128)(2,1)} %get-tuple-element.58) | data formatting | bytes 2359296
  172.1 0.9 copy.24
  173.0 0.9 copy.25
  173.9 0.9 copy.26
  (36 shorter events, 0.1 us)
Async XLA Ops:
  0.6 29.3 %collective-permute-start.1 = (bf16[768,768]{1,0:T(8,128)(2,1)}, bf16[768,768]{1,0:T(8,128)(2,1)}, u32[]{:S(2)}, u32[]{:S(2)}) collective-permute-start(bf16[768,768]{1,0:T(8,128)(2,1)} %param.10), channel_id=1, source_target_pairs={{0,2},{1,3},{2,0},{3,1},{4,6},{5,7},{6,4},{7,5},{8,10},{9,11},{10,... | collective-permute-start | bytes 3538952 | tf_op jit(solution)/shard_map/ppermute | solution.py:157
  3.7 46.0 %collective-permute-start = (bf16[768,768]{1,0:T(8,128)(2,1)}, bf16[768,768]{1,0:T(8,128)(2,1)}, u32[]{:S(2)}, u32[]{:S(2)}) collective-permute-start(bf16[768,768]{1,0:T(8,128)(2,1)} %param.10), channel_id=1, source_target_pairs={{0,1},{1,0},{2,3},{3,2},{4,5},{5,4},{6,7},{7,6},{8,9},{9,8},{10,11... | collective-permute-start | bytes 3538952 | tf_op jit(solution)/shard_map/ppermute | solution.py:157
  5.1 24.8 %copy-start.22 = (s32[2,4]{1,0:T(2,128)S(1)}, s32[2,4]{1,0:T(2,128)}, u32[]{:S(2)}) copy-start(s32[2,4]{1,0:T(2,128)} %param.11) | copy-start | bytes 100
  5.1 25.5 %copy-start.16 = (bf16[768,768]{1,0:T(8,128)(2,1)S(1)}, bf16[768,768]{1,0:T(8,128)(2,1)}, u32[]{:S(2)}) copy-start(bf16[768,768]{1,0:T(8,128)(2,1)} %param.10) | copy-start | bytes 3538948
  6.1 26.7 %collective-permute-start.3 = (bf16[2,768,256]{2,1,0:T(8,128)(2,1)}, bf16[2,768,256]{2,1,0:T(8,128)(2,1)S(1)}, u32[]{:S(2)}, u32[]{:S(2)}) collective-permute-start(bf16[2,768,256]{2,1,0:T(8,128)(2,1)} %pad_maximum_fusion.1), channel_id=1, source_target_pairs={{0,4},{4,0},{8,12},{12,8},{16,20},{20,16},{24,28},{28,24},{1,5},{5... | collective-permute-start | bytes 2359304 | tf_op jit(solution)/shard_map/ppermute | solution.py:157
  8.5 34.7 %collective-permute-start.5 = (bf16[2,768,256]{2,1,0:T(8,128)(2,1)}, bf16[2,768,256]{2,1,0:T(8,128)(2,1)}, u32[]{:S(2)}, u32[]{:S(2)}) collective-permute-start(bf16[2,768,256]{2,1,0:T(8,128)(2,1)} %pad_maximum_fusion.2), channel_id=1, source_target_pairs={{0,4},{4,0},{8,12},{12,8},{16,20},{20,16},{24,28},{28,24},{1,5},{5... | collective-permute-start | bytes 2359304 | tf_op jit(solution)/shard_map/ppermute | solution.py:157
  29.9 21.9 %collective-permute-start.2 = (bf16[768,768]{1,0:T(8,128)(2,1)}, bf16[768,768]{1,0:T(8,128)(2,1)S(1)}, u32[]{:S(2)}, u32[]{:S(2)}) collective-permute-start(bf16[768,768]{1,0:T(8,128)(2,1)} %collective-permute-done.1), channel_id=1, source_target_pairs={{0,1},{1,0},{2,3},{3,2},{4,5},{5,4},{6,7},{7,6},{8,9},{9,8},{10,11... | collective-permute-start | bytes 3538952 | tf_op jit(solution)/shard_map/ppermute | solution.py:157
  30.7 16.9 %copy-start.14 = (bf16[512,3072]{1,0:T(8,128)(2,1)S(1)}, bf16[512,3072]{1,0:T(8,128)(2,1)}, u32[]{:S(2)}) copy-start(bf16[512,3072]{1,0:T(8,128)(2,1)} %refs_3_.1) | copy-start | bytes 9437188
  32.8 16.9 %copy-start.12 = (bf16[2,768,256]{2,1,0:T(8,128)(2,1)}, bf16[2,768,256]{2,1,0:T(8,128)(2,1)S(1)}, u32[]{:S(2)}) copy-start(bf16[2,768,256]{2,1,0:T(8,128)(2,1)S(1)} %collective-permute-done.3.near) | copy-start | bytes 2359300
  32.8 26.0 %collective-permute-start.4 = (bf16[2,768,256]{2,1,0:T(8,128)(2,1)S(1)}, bf16[2,768,256]{2,1,0:T(8,128)(2,1)S(1)}, u32[]{:S(2)}, u32[]{:S(2)}) collective-permute-start(bf16[2,768,256]{2,1,0:T(8,128)(2,1)S(1)} %collective-permute-done.3.near), channel_id=1, source_target_pairs={{0,8},{8,16},{12,4},{16,24},{20,12},{28,20},{1,9},{9,17},{13,5},{1... | collective-permute-start | bytes 2359304 | tf_op jit(solution)/shard_map/ppermute | solution.py:163
  43.2 39.6 %collective-permute-start.6 = (bf16[2,768,256]{2,1,0:T(8,128)(2,1)}, bf16[2,768,256]{2,1,0:T(8,128)(2,1)}, u32[]{:S(2)}, u32[]{:S(2)}) collective-permute-start(bf16[2,768,256]{2,1,0:T(8,128)(2,1)} %collective-permute-done.5.near), channel_id=1, source_target_pairs={{0,8},{8,16},{12,4},{16,24},{20,12},{28,20},{1,9},{9,17},{13,5},{1... | collective-permute-start | bytes 2359304 | tf_op jit(solution)/shard_map/ppermute | solution.py:163
  51.8 1.0 copy-start.15
  56.5 2.3 %copy-start.7 = (bf16[768,512]{1,0:T(8,128)(2,1)S(1)}, bf16[768,512]{1,0:T(8,128)(2,1)}, u32[]{:S(2)}) copy-start(bf16[768,512]{1,0:T(8,128)(2,1)} %km.3) | copy-start | bytes 2359300
  56.5 2.3 %copy-start.8 = (bf16[768,512]{1,0:T(8,128)(2,1)S(1)}, bf16[768,512]{1,0:T(8,128)(2,1)}, u32[]{:S(2)}) copy-start(bf16[768,512]{1,0:T(8,128)(2,1)} %vm.3) | copy-start | bytes 2359300
  56.5 2.3 %copy-start.10 = (bf16[768,512]{1,0:T(8,128)(2,1)S(1)}, bf16[768,512]{1,0:T(8,128)(2,1)}, u32[]{:S(2)}) copy-start(bf16[768,512]{1,0:T(8,128)(2,1)} %q.3) | copy-start | bytes 2359300
  56.5 2.3 %copy-start.13 = (bf16[2,768,256]{2,1,0:T(8,128)(2,1)S(1)}, bf16[2,768,256]{2,1,0:T(8,128)(2,1)}, u32[]{:S(2)}) copy-start(bf16[2,768,256]{2,1,0:T(8,128)(2,1)} %copy-done.12) | copy-start | bytes 2359300
  73.1 1.1 copy-start
  74.2 1.2 copy-start.1
  75.4 0.8 copy-start.4
  76.2 5.1 %copy-start.5 = (bf16[2,768,256]{2,1,0:T(8,128)(2,1)}, bf16[2,768,256]{2,1,0:T(8,128)(2,1)S(1)}, u32[]{:S(2)}) copy-start(bf16[2,768,256]{2,1,0:T(8,128)(2,1)S(1)} %get-tuple-element.37.refs_4_) | copy-start | bytes 2359300
  81.3 21.1 %collective-permute-start.8 = (bf16[4,256,384]{2,1,0:T(8,128)(2,1)}, bf16[4,256,384]{2,1,0:T(8,128)(2,1)S(1)}, u32[]{:S(2)}, u32[]{:S(2)}) collective-permute-start(bf16[4,256,384]{2,1,0:T(8,128)(2,1)} %shard_map.102), channel_id=1, source_target_pairs={{0,4},{4,0},{8,12},{12,8},{16,20},{20,16},{24,28},{28,24},{1,5},{5... | collective-permute-start | bytes 2359304 | tf_op jit(solution)/shard_map/ppermute | solution.py:157
  81.3 21.1 %collective-permute-start.7 = (bf16[2,768,256]{2,1,0:T(8,128)(2,1)S(1)}, bf16[2,768,256]{2,1,0:T(8,128)(2,1)S(1)}, u32[]{:S(2)}, u32[]{:S(2)}) collective-permute-start(bf16[2,768,256]{2,1,0:T(8,128)(2,1)S(1)} %get-tuple-element.37.refs_4_), channel_id=1, source_target_pairs={{4,12},{8,0},{12,20},{16,8},{20,28},{24,16},{5,13},{9,1},{13,21},{... | collective-permute-start | bytes 2359304 | tf_op jit(solution)/shard_map/ppermute | solution.py:163
  82.8 1.1 copy-start.11
  99.0 1.2 copy-start.2
  100.1 1.2 copy-start.3
  101.4 1.1 copy-start.6
  101.4 1.3 copy-start.9
  102.4 0.9 copy-start.17
  102.5 1.0 copy-start.18
  169.6 2.5 %copy-start.21 = (bf16[768,512]{1,0:T(8,128)(2,1)S(1)}, bf16[768,512]{1,0:T(8,128)(2,1)}, u32[]{:S(2)}) copy-start(bf16[768,512]{1,0:T(8,128)(2,1)} %get-tuple-element.60) | copy-start | bytes 2359300
  169.6 3.4 %copy-start.20 = (bf16[768,512]{1,0:T(8,128)(2,1)S(1)}, bf16[768,512]{1,0:T(8,128)(2,1)}, u32[]{:S(2)}) copy-start(bf16[768,512]{1,0:T(8,128)(2,1)} %get-tuple-element.61) | copy-start | bytes 2359300
  172.1 1.8 %copy-start.19 = (f32[512,384]{1,0:T(8,128)S(1)}, f32[512,384]{1,0:T(8,128)}, u32[]{:S(2)}) copy-start(f32[512,384]{1,0:T(8,128)} %get-tuple-element.62) | copy-start | bytes 2359300
